TPU v7x, 32 devices: a whole 2x2x4 slice. The times are simulated.
32 devices in a mesh: dp: 16 (over z, x, core), mp: 2 (over y).
Axes of the slice: x: 2, y: 2, z: 4, core: 2. Of those that a mesh axis runs over, the one named last changes fastest.
Arguments:
- inputs: bfloat16 [32768, 768], P(('dp', 'mp')), may hold values from -12 to 12
- segments: int32 [32768], P('dp'), may hold values from -1 to 9, as said below
- w_qkv: bfloat16 [3, 768, 768], P(None, 'dp', 'mp'), may hold values from -0.21875 to 0.21875
- w_out: bfloat16 [768, 768], P('mp', 'dp'), may hold values from -4 to 4
- first_gain: bfloat16 [768], P('dp'), may hold values from 0.5 to 1.5
- first_bias: bfloat16 [768], P('dp'), may hold values from -3 to 3
- w_gate: bfloat16 [768, 3072], P('dp', 'mp'), may hold values from -0.21875 to 0.21875
- w_up: bfloat16 [768, 3072], P('dp', 'mp'), may hold values from -0.21875 to 0.21875
- w_down: bfloat16 [3072, 768], P('mp', 'dp'), may hold values from -0.109375 to 0.109375
- second_gain: bfloat16 [768], P('dp'), may hold values from 0.5 to 1.5
- second_bias: bfloat16 [768], P('dp'), may hold values from -3 to 3
- d_out: bfloat16 [32768, 768], P(('dp', 'mp')), may hold values from -12 to 12
Outputs:
- outputs: bfloat16 [32768, 768], P(('dp', 'mp'))
- grad_inputs: float32 [32768, 768], P(('dp', 'mp'))
- grad_w_qkv: float32 [3, 768, 768], P(None, 'dp', 'mp')
- grad_w_out: float32 [768, 768], P('mp', 'dp')
- grad_first_gain: float32 [768], P('dp')
- grad_first_bias: float32 [768], P('dp')
- grad_w_gate: float32 [768, 3072], P('dp', 'mp')
- grad_w_up: float32 [768, 3072], P('dp', 'mp')
- grad_w_down: float32 [3072, 768], P('mp', 'dp')
- grad_second_gain: float32 [768], P('dp')
- grad_second_bias: float32 [768], P('dp')
Inputs may be any that keep to these rules, and one draw needn't show every extreme that they name: `segments`: within each sequence of 2048 tokens, tokens carry the number of their document, counting from 0 in order; each document has 200 to 2000 tokens; the tokens after the last whole document are padding, marked -1, and every sequence ends with one or more of them. In the first sequence every document has exactly 200 tokens.
All inputs are finite; a program needn't handle non-finite values.
Results may differ from a plain program's by a relative error of at most 0.017.
The roundings to bfloat16 on the way count: a program that leaves them out, or rounds other values in their place, can miss the bound.
Values may be sent and summed in bfloat16 or wider, within the bound.
A program may use at most 192 MiB of HBM per device.

v0:
```python
import functools

import jax
import jax.numpy as jnp
import numpy as np
from jax import lax
from jax.experimental import pallas as pl
from jax.experimental.pallas import tpu as pltpu
from jax.sharding import Mesh
from jax.sharding import PartitionSpec as P

HEAD_DIM = 64
SEQ_LEN = 2048
LANES = 128
EPSILON = 1e-12
ROPE_BASE = 1000.0
MASKED = -10000.0
SCALE = HEAD_DIM**-0.5
F32 = jnp.float32
BF16 = jnp.bfloat16
NT = (((1,), (1,)), ((), ()))
NN = (((1,), (0,)), ((), ()))
TN = (((0,), (0,)), ((), ()))
VMEM_BYTES = 60 << 20
FEED_VMEM = 62 << 20
FWD_Q, FWD_K = 1024, 512
BWD_Q, BWD_K = 1024, 512
ROW_BLOCK = 256
MESH_ID = pl.DeviceIdType.MESH
LINE = 4
FIRST_TILES = 2
ROW_PARTS = LINE


def dot(left, right, dims=NN):
    return lax.dot_general(left, right, dims, preferred_element_type=F32)


def rope_tables():
    half = HEAD_DIM // 2
    frequency = ROPE_BASE ** (-2.0 * np.arange(half) / HEAD_DIM)
    angles = np.arange(SEQ_LEN)[:, None] * frequency[None, :]
    cos, sin = np.cos(angles), np.sin(angles)
    heads = LANES // HEAD_DIM
    return (
        np.tile(np.concatenate([cos, cos], 1), (1, heads)).astype(np.float32),
        np.tile(np.concatenate([-sin, sin], 1), (1, heads)).astype(np.float32),
    )


def half_swap(tile):
    lane = lax.broadcasted_iota(jnp.int32, (1, LANES), 1)
    half = HEAD_DIM // 2
    return jnp.where(
        lane % HEAD_DIM < half,
        pltpu.roll(tile, LANES - half, 1),
        pltpu.roll(tile, half, 1),
    )


def project_kernel(core_ref, x_ref, w_ref, cos_ref, sin_ref, out_ref, *, pairs):
    x = x_ref[...]
    cos, sin = cos_ref[...], sin_ref[...]
    for pair in range(pairs):
        base = pair * 3 * LANES
        tile = dot(x, w_ref[0, :, base : base + 3 * LANES])
        for kind in range(2):
            part = tile[:, kind * LANES : (kind + 1) * LANES]
            out_ref[:, base + kind * LANES : base + (kind + 1) * LANES] = (
                part * cos + half_swap(part) * sin
            ).astype(BF16)
        out_ref[:, base + 2 * LANES : base + 3 * LANES] = tile[:, 2 * LANES :].astype(BF16)


def project(core, rows, weights, cos, sin):
    tokens, depth = rows.shape
    wide = weights.shape[2]
    steps = tokens // ROW_BLOCK

    def turned(step, core_ref):
        return (lax.rem(step + core_ref[0] * (steps // 2), steps), 0)

    return pl.pallas_call(
        functools.partial(project_kernel, pairs=wide // (3 * LANES)),
        grid_spec=pltpu.PrefetchScalarGridSpec(
            num_scalar_prefetch=1,
            grid=(steps,),
            in_specs=[
                pl.BlockSpec((ROW_BLOCK, depth), lambda i, c: (i, 0)),
                pl.BlockSpec((1, depth, wide), lambda i, c: (c[0], 0, 0)),
                pl.BlockSpec((ROW_BLOCK, LANES), turned),
                pl.BlockSpec((ROW_BLOCK, LANES), turned),
            ],
            out_specs=pl.BlockSpec((ROW_BLOCK, wide), lambda i, c: (i, 0)),
        ),
        out_shape=jax.ShapeDtypeStruct((tokens, wide), BF16),
        compiler_params=pltpu.CompilerParams(vmem_limit_bytes=VMEM_BYTES),
        cost_estimate=pl.CostEstimate(
            flops=2 * tokens * depth * wide,
            bytes_accessed=2 * tokens * (depth + wide) + 2 * depth * wide,
            transcendentals=0,
        ),
        name="project",
    )(core, rows, weights, cos, sin)


def block_range(labels, block, other, turn):
    blocks = labels.shape[0] // block
    valid = labels >= 0
    tiles = labels.reshape(blocks, block)
    first, last = tiles[:, 0], jnp.max(tiles, axis=1)
    low = jnp.sum((valid[None] & (labels[None] < first[:, None])).astype(jnp.int32), 1)
    high = jnp.sum((valid[None] & (labels[None] <= last[:, None])).astype(jnp.int32), 1)
    offset = (labels.shape[0] - turn) // other
    return low // other + offset, jnp.where(high > low, (high + other - 1) // other, low // other) + offset


def attend_kernel(low_ref, high_ref, q_ref, k_ref, v_ref, key_ref, query_ref, o_ref, lse_ref, v_turned):
    tokens = q_ref.shape[0]
    key_blocks = tokens // FWD_K
    lane = lax.broadcasted_iota(jnp.int32, (1, LANES), 1)
    zero = jnp.zeros((), BF16)
    v_turned[...] = v_ref[...].T

    @pl.loop(0, tokens // FWD_Q)
    def _(i):
        q0 = pl.multiple_of(i * FWD_Q, FWD_Q)
        scaled = q_ref[pl.ds(q0, FWD_Q), :] * jnp.asarray(SCALE, BF16)
        halves = (
            jnp.where(lane < HEAD_DIM, scaled, zero),
            jnp.where(lane >= HEAD_DIM, scaled, zero),
        )
        query_label = query_ref[:, pl.ds(q0, FWD_Q)]

        def body(j, carry):
            k0 = pl.multiple_of(lax.rem(j, key_blocks) * FWD_K, FWD_K)
            k = k_ref[pl.ds(k0, FWD_K), :]
            same = key_ref[pl.ds(k0, FWD_K), :] == query_label
            scores = [dot(k, half, NT) for half in halves]
            out = []
            for h in range(2):
                top, total, acc = carry[h]
                s = jnp.where(same, scores[h], -1e30)
                new_top = jnp.maximum(top, jnp.max(s, axis=0, keepdims=True))
                fade = jnp.exp(top - new_top)
                e = jnp.exp(s - new_top)
                total = fade * total + jnp.sum(e, axis=0, keepdims=True)
                part = dot(v_turned[h * HEAD_DIM : (h + 1) * HEAD_DIM, pl.ds(k0, FWD_K)], e.astype(BF16))
                out.append((new_top, total, acc * fade + part))
            return tuple(out)

        start = (
            jnp.full((1, FWD_Q), MASKED, F32),
            jnp.zeros((1, FWD_Q), F32),
            jnp.zeros((HEAD_DIM, FWD_Q), F32),
        )
        ended = lax.fori_loop(low_ref[i], high_ref[i], body, (start, start))
        out = []
        for h in range(2):
            top, total, acc = ended[h]
            norm = jnp.maximum(total, 1.0)
            out.append(acc / norm)
            lse_ref[0, pl.ds(h, 1), pl.ds(q0, FWD_Q)] = top + jnp.log(norm)
        o_ref[pl.ds(q0, FWD_Q), :] = jnp.concatenate(out, 0).T.astype(BF16)


def attend(qkv, labels, turn):
    tokens = qkv.shape[0]
    pairs = qkv.shape[1] // (3 * LANES)
    low, high = block_range(labels, FWD_Q, FWD_K, turn)
    queries = jnp.where(labels < 0, -2, labels)
    whole = lambda shape: pl.BlockSpec(shape, lambda p, *_: (0,) * len(shape))
    part = lambda kind: pl.BlockSpec((tokens, LANES), lambda p, *_: (0, 3 * p + kind))
    return pl.pallas_call(
        attend_kernel,
        grid_spec=pltpu.PrefetchScalarGridSpec(
            num_scalar_prefetch=2,
            grid=(pairs,),
            in_specs=[part(0), part(1), part(2), whole((tokens, 1)), whole((1, tokens))],
            out_specs=[
                pl.BlockSpec((tokens, LANES), lambda p, *_: (0, p)),
                pl.BlockSpec((1, 2, tokens), lambda p, *_: (p, 0, 0)),
            ],
            scratch_shapes=[pltpu.VMEM((LANES, tokens), BF16)],
        ),
        out_shape=[
            jax.ShapeDtypeStruct((tokens, pairs * LANES), BF16),
            jax.ShapeDtypeStruct((pairs, 2, tokens), F32),
        ],
        compiler_params=pltpu.CompilerParams(vmem_limit_bytes=VMEM_BYTES),
        cost_estimate=pl.CostEstimate(
            flops=pairs * 8 * tokens * tokens * LANES,
            bytes_accessed=pairs * 4 * tokens * LANES * 2,
            transcendentals=pairs * 2 * tokens * tokens,
        ),
        name="attend",
    )(low, high, qkv, qkv, qkv, labels[:, None], queries[None])


def attend_back_step(t, refs, scratch):
    q_all, o_all, do_all, lse_ref, key_ref, query_ref, cos_ref, sin_ref, out_ref = refs
    dq_turned, inner, k_turned = scratch
    tokens = q_all.shape[0]
    blocks = tokens // BWD_K
    pair, j = t // blocks, lax.rem(t, blocks)
    lane = lax.broadcasted_iota(jnp.int32, (1, LANES), 1)
    zero = jnp.zeros((), BF16)
    picks = (lane < HEAD_DIM, lane >= HEAD_DIM)

    def lanes(kind):
        return pl.ds(pl.multiple_of((pair * 3 + kind) * LANES, LANES), LANES)

    own = pl.ds(pl.multiple_of(pair * LANES, LANES), LANES)

    def unrope(tile, rows):
        return (tile * cos_ref[rows, :] - half_swap(tile) * sin_ref[rows, :]).astype(BF16)

    @pl.when(j == 0)
    def _():
        k_turned[...] = q_all[:, lanes(1)].T
        product = (o_all[:, own].astype(F32) * do_all[:, own].astype(F32)).T
        inner[0:1, :] = jnp.sum(product[:HEAD_DIM], axis=0, keepdims=True)
        inner[1:2, :] = jnp.sum(product[HEAD_DIM:], axis=0, keepdims=True)
        dq_turned[...] = jnp.zeros_like(dq_turned)

    key_rows = pl.ds(pl.multiple_of(j * BWD_K, BWD_K), BWD_K)
    key_label = key_ref[key_rows, :]
    dks, dvs = [], []
    for h in range(2):
        k = jnp.where(picks[h], q_all[key_rows, lanes(1)], zero)
        v = jnp.where(picks[h], q_all[key_rows, lanes(2)], zero)
        kt = k_turned[pl.ds(h * HEAD_DIM, HEAD_DIM), key_rows]

        def body(i, carry):
            dk, dv = carry
            query_rows = pl.ds(pl.multiple_of(i * BWD_Q, BWD_Q), BWD_Q)
            q = q_all[query_rows, lanes(0)]
            do = do_all[query_rows, own]
            s = dot(k, q, NT)
            p = jnp.exp(s * SCALE - lse_ref[pair, pl.ds(h, 1), query_rows])
            p = jnp.where(key_label == query_ref[:, query_rows], p, 0.0)
            dp = dot(v, do, NT)
            ds = (p * (dp - inner[pl.ds(h, 1), query_rows])).astype(BF16)
            dv = dv + dot(p.astype(BF16), do)
            dk = dk + dot(ds, q)
            dq_turned[pl.ds(h * HEAD_DIM, HEAD_DIM), query_rows] += dot(kt, ds)
            return dk, dv

        empty = jnp.zeros((BWD_K, LANES), F32)
        dk, dv = lax.fori_loop(0, tokens // BWD_Q, body, (empty, empty))
        dks.append(dk)
        dvs.append(dv)
    out_ref[key_rows, lanes(1)] = unrope(jnp.where(picks[0], dks[0], dks[1]) * SCALE, key_rows)
    out_ref[key_rows, lanes(2)] = jnp.where(picks[0], dvs[0], dvs[1]).astype(BF16)

    @pl.when(j == blocks - 1)
    def _():
        out_ref[:, lanes(0)] = unrope(dq_turned[...].T * SCALE, pl.ds(0, tokens))


def attend_back_kernel(*refs, remote):
    refs, steps = list(refs), refs[0].shape[0] // BWD_K * (refs[0].shape[1] // (3 * LANES))
    inputs, refs = refs[:9], refs[9:]
    do_all, do_sem, scratch = refs[-2], refs[-1], None
    refs = refs[:-2]
    half = inputs[2].shape[0]
    takes = [
        pltpu.make_async_copy(inputs[2 + k], do_all.at[pl.ds(k * half, half)], do_sem.at[k]) for k in range(2)
    ]
    inputs = [*inputs[:2], do_all, *inputs[4:]]
    for take in takes:
        take.start()
    if not remote:
        out_ref, scratch = refs[0], refs[1:]
        for take in takes:
            take.wait()

        @pl.loop(0, steps)
        def _(t):
            attend_back_step(t, (*inputs, out_ref), scratch)

        return
    grads, out_ref, sums, scratch = refs[0], refs[1], refs[2], refs[3:]
    greet(False)
    reduce = Reduce(grads, sums, scratch[3:])
    reduce.begin()
    for take in takes:
        take.wait()

    @pl.loop(0, max(steps, reduce.STEPS))
    def _(t):
        reduce.step(t)

        @pl.when(t < steps)
        def _():
            attend_back_step(t, (*inputs, out_ref), scratch[:3])

    reduce.end()


def attend_back(qkv, o, do, do_in, lse, labels, cos, sin, grads, devices, collective_id):
    tokens, wide = qkv.shape
    remote = devices == 8 * LINE
    queries = jnp.where(labels < 0, -2, labels)
    vmem = pl.BlockSpec(memory_space=pltpu.VMEM)
    operands = [qkv, o, do, do_in, lse, labels[:, None], queries[None], cos, sin]
    out_shape = [jax.ShapeDtypeStruct((tokens, wide), BF16)]
    scratch = [
        pltpu.VMEM((LANES, tokens), F32),
        pltpu.VMEM((8, tokens), F32),
        pltpu.VMEM((LANES, tokens), BF16),
    ]
    anywhere = pl.BlockSpec(memory_space=pl.ANY)
    in_specs = [vmem, vmem, anywhere, anywhere] + [vmem] * 5
    params = dict(vmem_limit_bytes=VMEM_BYTES)
    if remote:
        rows, width = 2 * grads.shape[1] // devices, grads.shape[2]
        operands.append(grads)
        in_specs.append(pl.BlockSpec(memory_space=pl.ANY))
        out_shape.append(jax.ShapeDtypeStruct((rows, width), F32))
        scratch += Reduce.scratch(rows, width, (width // LANES + 1) // 2 * LANES)
        params.update(collective_id=collective_id, has_side_effects=True)
    scratch += [pltpu.VMEM((tokens, wide // 3), BF16), pltpu.SemaphoreType.DMA((2,))]
    out = pl.pallas_call(
        functools.partial(attend_back_kernel, remote=remote),
        in_specs=in_specs,
        out_specs=[vmem] * len(out_shape),
        out_shape=out_shape,
        scratch_shapes=scratch,
        compiler_params=pltpu.CompilerParams(**params),
        cost_estimate=pl.CostEstimate(
            flops=wide // (3 * LANES) * 20 * tokens * tokens * LANES,
            bytes_accessed=8 * tokens * wide,
            transcendentals=wide // (3 * LANES) * 2 * tokens * tokens,
        ),
        name="attend_back",
    )(*operands)
    return (out[0], out[1]) if remote else (out[0], scatter_sum(grads))


def scatter_sum(grads):
    flat = grads.reshape(-1, grads.shape[2])
    return lax.psum_scatter(flat, ("mp", "chip", "core"), scatter_dimension=0, tiled=True).astype(F32)


def place():
    chip = lax.axis_index("chip")
    return chip // 2, lax.rem(chip, 2), lax.axis_index("core"), lax.axis_index("mp")


def target(a, b, core, y):
    return {"chip": a * 2 + b, "core": core, "mp": y}


def greet(moves):
    a, b, core, y = place()
    barrier = pltpu.get_barrier_semaphore()

    def signal(device):
        pl.semaphore_signal(barrier, inc=1, device_id=device, device_id_type=MESH_ID)

    signal(target(a, 1 - b, core, y))
    signal(target(a, b, core, 1 - y))
    signal(target(a, b, 1 - core, y))

    @pl.when(a > 0)
    def _():
        signal(target(a - 1, b, core, y))

    @pl.when(a < LINE - 1)
    def _():
        signal(target(a + 1, b, core, y))

    @pl.when(moves)
    def _():
        signal(target(a, b, y, core))

    edges = jnp.where(a > 0, 1, 0) + jnp.where(a < LINE - 1, 1, 0) + jnp.where(moves, 1, 0)
    pl.semaphore_wait(barrier, 3 + edges)


class Gather:
    def __init__(self, src, dst, send, recv, local):
        self.src, self.dst, self.send, self.recv, self.local = src, dst, send, recv, local
        self.rows, self.width = src.shape
        tiles = self.width // LANES
        first = FIRST_TILES * LANES if FIRST_TILES < tiles else tiles // 2 * LANES
        self.columns = [(0, first), (first, self.width - first)]
        self.a, self.b, self.core, self.y = place()

    def span(self, half):
        start, size = (0, self.width) if half is None else self.columns[half]
        return pl.ds(start, size)

    def at(self, piece, core=None):
        pa, pb, py, half = piece
        core = self.core if core is None else core
        row = pl.multiple_of(((pa * 2 + pb) * 2 + core) * self.rows, self.rows)
        return self.dst.at[py, pl.ds(row, self.rows), self.span(half)]

    def own_copy(self):
        return pltpu.make_async_copy(self.src, self.at((self.a, self.b, self.y, None)), self.local)

    def start(self, piece, slot, device, mine=False):
        source = self.src.at[:, self.span(piece[3])] if mine else self.at(piece)
        pltpu.make_async_remote_copy(
            source, self.at(piece), self.send.at[slot], self.recv.at[slot], device_id=device, device_id_type=MESH_ID
        ).start()

    def handle(self, piece, slot, core=None):
        ref = self.at(piece, core)
        return pltpu.make_async_remote_copy(
            ref,
            ref,
            self.send.at[slot],
            self.recv.at[slot],
            device_id=target(self.a, self.b, 1 - self.core, self.y),
            device_id_type=MESH_ID,
        )

    def arrived(self, piece, slot, core=None):
        self.handle(piece, slot, core).wait_recv()

    def sent(self, piece, slot):
        self.handle(piece, slot).wait_send()

    def to_x(self, piece, slot, mine=False):
        self.start(piece, slot, target(self.a, 1 - self.b, self.core, self.y), mine)

    def to_y(self, piece, slot, mine=False):
        self.start(piece, slot, target(self.a, self.b, self.core, 1 - self.y), mine)

    def to_mate(self, piece, slot, mine=False):
        self.start(piece, slot, target(self.a, self.b, 1 - self.core, self.y), mine)

    def to_line(self, piece, slot, step, mine=False):
        self.start(piece, slot, target(self.a + step, self.b, self.core, self.y), mine)

    def spread(self, pa, rank, mine=False):
        b, y = self.b, self.y
        self.to_x((pa, b, y, 0), 6 + rank, mine)
        self.to_y((pa, b, y, 1), 18 + rank, mine)
        for half in range(2):
            self.to_mate((pa, b, y, half), 30 + 2 * rank + half, mine)
        self.to_y((pa, b, y, 0), 22 + rank, mine)
        self.to_x((pa, b, y, 1), 10 + rank, mine)

    def begin(self):
        a, b, y = self.a, self.b, self.y
        piece = (a, b, y, None)

        @pl.when(a < LINE - 1)
        def _():
            self.to_line(piece, 0, 1, True)

        @pl.when(a > 0)
        def _():
            self.to_line(piece, 3, -1, True)

        self.spread(a, 0, True)
        self.own_copy().start()

    def hop(self, h):
        a, b, y = self.a, self.b, self.y

        @pl.when(a - h >= 0)
        def _():
            self.arrived((a - h, b, y, None), h - 1)
            if h < LINE - 1:

                @pl.when(a < LINE - 1)
                def _():
                    self.to_line((a - h, b, y, None), h, 1)

            self.spread(a - h, LINE - h)

        @pl.when(a + h < LINE)
        def _():
            self.arrived((a + h, b, y, None), 2 + h)
            if h < LINE - 1:

                @pl.when(a > 0)
                def _():
                    self.to_line((a + h, b, y, None), 3 + h, -1)

            self.spread(a + h, h)

    def ranks(self):
        return [(rank, lax.rem(self.a + rank, LINE)) for rank in range(LINE)]

    def turn(self):
        b, y = self.b, self.y
        for rank, pa in self.ranks():
            self.arrived((pa, 1 - b, y, 0), 6 + rank)
            self.to_y((pa, 1 - b, y, 0), 26 + rank)
            self.to_mate((pa, 1 - b, y, 0), 38 + rank)
            self.arrived((pa, b, 1 - y, 1), 18 + rank)
            self.to_x((pa, b, 1 - y, 1), 14 + rank)
            self.to_mate((pa, b, 1 - y, 1), 42 + rank)

    def last(self):
        b, y = self.b, self.y
        for rank, pa in self.ranks():
            for far in range(2):
                pb, py = (b, 1 - b)[far], (y, 1 - y)[far]
                self.arrived((pa, pb, 1 - y, 0), 22 + 4 * far + rank)
                self.to_mate((pa, pb, 1 - y, 0), 46 + 4 * far + rank)
                self.arrived((pa, 1 - b, py, 1), 10 + 4 * far + rank)
                self.to_mate((pa, 1 - b, py, 1), 54 + 4 * far + rank)

    def end(self):
        a, b, y = self.a, self.b, self.y
        other = 1 - self.core
        for rank, pa in self.ranks():
            pieces = [((pa, b, y, 0), 30 + 2 * rank), ((pa, b, y, 1), 31 + 2 * rank)]
            pieces += [((pa, 1 - b, y, 0), 38 + rank), ((pa, b, 1 - y, 1), 42 + rank)]
            for far in range(2):
                pb, py = (b, 1 - b)[far], (y, 1 - y)[far]
                pieces += [((pa, pb, 1 - y, 0), 46 + 4 * far + rank), ((pa, 1 - b, py, 1), 54 + 4 * far + rank)]
            for piece, slot in pieces:
                self.arrived(piece, slot, other)
                self.sent(piece, slot)
            self.sent((pa, b, y, 0), 6 + rank)
            self.sent((pa, b, y, 1), 18 + rank)
            self.sent((pa, b, y, 1), 10 + rank)
            self.sent((pa, b, 1 - y, 1), 14 + rank)
            self.sent((pa, b, y, 0), 22 + rank)
            self.sent((pa, 1 - b, y, 0), 26 + rank)

        @pl.when(a < LINE - 1)
        def _():
            self.sent((a, b, y, None), 0)

        @pl.when(a > 0)
        def _():
            self.sent((a, b, y, None), 3)

        for h in range(1, LINE - 1):

            @pl.when((a - h >= 0) & (a < LINE - 1))
            def _():
                self.sent((a - h, b, y, None), h)

            @pl.when((a + h < LINE) & (a > 0))
            def _():
                self.sent((a + h, b, y, None), 3 + h)

        self.own_copy().wait()


def enter_kernel(src, rows, dst, rows_all, copy_send, copy_recv, local, row_send, row_recv, held):
    a, b, core, y = place()
    half = rows.shape[0]
    part = half // ROW_PARTS
    moves = core != y
    greet(moves)

    def crossing(k):
        span = pl.ds(k * part, part)
        return pltpu.make_async_remote_copy(
            rows.at[span],
            rows_all.at[span],
            row_send.at[0, k],
            row_recv.at[0, k],
            device_id=target(a, b, y, core),
            device_id_type=MESH_ID,
        )

    def to_mate(source, k):
        return pltpu.make_async_remote_copy(
            source.at[pl.ds(k * part, part)],
            rows_all.at[pl.ds(half + k * part, part)],
            row_send.at[1, k],
            row_recv.at[1, k],
            device_id=target(a, b, 1 - core, y),
            device_id_type=MESH_ID,
        )

    take = pltpu.make_async_copy(rows, held, row_recv.at[2, 0])
    stay = pltpu.make_async_copy(held, rows_all.at[pl.ds(0, half)], row_recv.at[2, 1])

    def send(k):
        @pl.when(moves)
        def _():
            crossing(k).start()

        @pl.when(jnp.logical_not(moves))
        def _():
            to_mate(rows, k).start()

    @pl.when(jnp.logical_not(moves))
    def _():
        take.start()

    def hand_on(k):
        @pl.when(moves)
        def _():
            crossing(k).wait()
            to_mate(rows_all, k).start()

    gather = Gather(src, dst, copy_send, copy_recv, local)
    gather.begin()
    send(0)

    @pl.when(jnp.logical_not(moves))
    def _():
        take.wait()
        stay.start()

    for h in range(1, LINE):
        gather.hop(h)
        send(h)
    hand_on(0)
    hand_on(1)
    gather.turn()
    hand_on(2)
    hand_on(3)
    gather.last()

    @pl.when(jnp.logical_not(moves))
    def _():
        stay.wait()

    for k in range(ROW_PARTS):
        to_mate(rows_all, k).wait()
    gather.end()


def enter(shard, rows, devices, cross, mate, collective_id):
    shard_rows, width = shard.shape
    if devices != 2 * 2 * 2 * LINE:
        weights = lax.all_gather(shard, ("mp", "chip", "core"), axis=0, tiled=True)
        own = cross(rows)
        return weights.reshape(2, -1, width), jnp.concatenate([own, mate(own)], axis=0)
    anywhere = pl.BlockSpec(memory_space=pl.ANY)
    return pl.pallas_call(
        enter_kernel,
        out_shape=[
            jax.ShapeDtypeStruct((2, devices // 2 * shard_rows, width), shard.dtype),
            jax.ShapeDtypeStruct((2 * rows.shape[0], rows.shape[1]), rows.dtype),
        ],
        in_specs=[anywhere, anywhere],
        out_specs=[anywhere, anywhere],
        scratch_shapes=[
            pltpu.SemaphoreType.DMA((62,)),
            pltpu.SemaphoreType.DMA((62,)),
            pltpu.SemaphoreType.DMA,
            pltpu.SemaphoreType.DMA((2, ROW_PARTS)),
            pltpu.SemaphoreType.DMA((3, ROW_PARTS)),
            pltpu.VMEM(rows.shape, rows.dtype),
        ],
        compiler_params=pltpu.CompilerParams(collective_id=collective_id, has_side_effects=True),
        name="enter",
    )(shard, rows)


class Reduce:
    STEPS = 14

    def __init__(self, src, out, scratch):
        self.src, self.out = src, out
        (
            self.acc,
            self.mates,
            self.y_two,
            self.x_two,
            self.x_one,
            self.y_one,
            self.up,
            self.down,
            self.load_sem,
            self.mate_send,
            self.mate_recv,
            self.y_send,
            self.y_recv,
            self.x_send,
            self.x_recv,
            self.up_send,
            self.up_recv,
            self.down_send,
            self.down_recv,
        ) = scratch
        self.rows, self.width = self.acc.shape[3:]
        self.first = self.y_two.shape[3]
        self.a, self.b, self.core, self.y = place()

    @staticmethod
    def scratch(rows, width, first):
        dma = pltpu.SemaphoreType.DMA
        return [
            pltpu.VMEM((LINE, 2, 2, rows, width), BF16),
            pltpu.VMEM((LINE, 2, 2, rows, width), BF16),
            pltpu.VMEM((LINE, 2, rows, first), BF16),
            pltpu.VMEM((LINE, 2, rows, width - first), BF16),
            pltpu.VMEM((LINE, rows, first), BF16),
            pltpu.VMEM((LINE, rows, width - first), BF16),
            pltpu.VMEM((LINE, rows, width), BF16),
            pltpu.VMEM((LINE, rows, width), BF16),
            dma((LINE, 2, 2)),
            dma((LINE, 2, 2)),
            dma((LINE, 2, 2)),
            dma((LINE, 3)),
            dma((LINE, 3)),
            dma((LINE, 3)),
            dma((LINE, 3)),
            dma((LINE,)),
            dma((LINE,)),
            dma((LINE,)),
            dma((LINE,)),
        ]

    def owner(self, group):
        near = jnp.where(self.a < LINE // 2, LINE - 1 - group, group)
        inner = [[3, 0, 2, 1], [0, 3, 1, 2]]
        pick = lambda order: sum(jnp.where(group == g, order[g], 0) for g in range(LINE))
        return jnp.where(self.a == 1, pick(inner[0]), jnp.where(self.a == 2, pick(inner[1]), near))

    def remote(self, src, dst, send, recv, device):
        return pltpu.make_async_remote_copy(src, dst, send, recv, device_id=device, device_id_type=MESH_ID)

    def source(self, group, pb, py, core):
        row = pl.multiple_of(((self.owner(group) * 2 + pb) * 2 + core) * self.rows, self.rows)
        return self.src.at[py, pl.ds(row, self.rows), :]

    def load(self, group, pb, py):
        return pltpu.make_async_copy(
            self.source(group, pb, py, self.core), self.acc.at[group, pb, py], self.load_sem.at[group, pb, py]
        )

    def to_mate(self, group, pb, py):
        return self.remote(
            self.source(group, pb, py, 1 - self.core),
            self.mates.at[group, pb, py],
            self.mate_send.at[group, pb, py],
            self.mate_recv.at[group, pb, py],
            target(self.a, self.b, 1 - self.core, self.y),
        )

    def low(self):
        return pl.ds(0, self.first)

    def high(self):
        return pl.ds(self.first, self.width - self.first)

    def over_y(self, group, k):
        device = target(self.a, self.b, self.core, 1 - self.y)
        if k < 2:
            src, dst = self.acc.at[group, k, 1 - self.y, :, self.low()], self.y_two.at[group, k]
        else:
            src, dst = self.acc.at[group, self.b, 1 - self.y, :, self.high()], self.y_one.at[group]
        return self.remote(src, dst, self.y_send.at[group, k], self.y_recv.at[group, k], device)

    def over_x(self, group, k):
        device = target(self.a, 1 - self.b, self.core, self.y)
        if k < 2:
            src, dst = self.acc.at[group, 1 - self.b, k, :, self.high()], self.x_two.at[group, k]
        else:
            src, dst = self.acc.at[group, 1 - self.b, self.y, :, self.low()], self.x_one.at[group]
        return self.remote(src, dst, self.x_send.at[group, k], self.x_recv.at[group, k], device)

    def along(self, group, step):
        pa = self.owner(group)
        src = self.acc.at[group, self.b, self.y]
        device = target(self.a + step, self.b, self.core, self.y)
        buffer, send, recv = (
            (self.up, self.up_send, self.up_recv) if step > 0 else (self.down, self.down_send, self.down_recv)
        )
        return self.remote(src, buffer.at[pa], send.at[pa], recv.at[pa], device)

    def add(self, ref, other):
        tile = 16

        @pl.loop(0, self.rows // tile)
        def _(i):
            span = pl.ds(pl.multiple_of(i * tile, tile), tile)
            ref[span, :] += other[span, :]

    def begin(self):
        for group in range(LINE):
            for pb in range(2):
                for py in range(2):
                    self.to_mate(group, pb, py).start()
                    self.load(group, pb, py).start()

    def first_stage(self, group):
        for pb in range(2):
            for py in range(2):
                self.load(group, pb, py).wait()
                self.to_mate(group, pb, py).wait_recv()
                self.add(self.acc.at[group, pb, py], self.mates.at[group, pb, py])
        for k in range(2):
            self.over_y(group, k).start()
            self.over_x(group, k).start()

    def second_stage(self, group):
        for k in range(2):
            self.over_y(group, k).wait_recv()
            self.add(self.acc.at[group, k, self.y, :, self.low()], self.y_two.at[group, k])
            self.over_x(group, k).wait_recv()
            self.add(self.acc.at[group, self.b, k, :, self.high()], self.x_two.at[group, k])
        self.over_x(group, 2).start()
        self.over_y(group, 2).start()

    def third_stage(self, group):
        mine = self.acc.at[group, self.b, self.y]
        self.over_x(group, 2).wait_recv()
        self.add(mine.at[:, self.low()], self.x_one.at[group])
        self.over_y(group, 2).wait_recv()
        self.add(mine.at[:, self.high()], self.y_one.at[group])
        pa = self.owner(group)

        @pl.when((self.a == 0) & (pa > 0))
        def _():
            self.along(group, 1).start()

        @pl.when((self.a == LINE - 1) & (pa < LINE - 1))
        def _():
            self.along(group, -1).start()

    def line_stage(self, group):
        mine = self.acc.at[group, self.b, self.y]
        pa = self.owner(group)

        @pl.when((self.a > 0) & (pa > self.a))
        def _():
            self.along(group, 1).wait_recv()
            self.add(mine, self.up.at[pa])
            self.along(group, 1).start()

        @pl.when((self.a < LINE - 1) & (pa < self.a))
        def _():
            self.along(group, -1).wait_recv()
            self.add(mine, self.down.at[pa])
            self.along(group, -1).start()

    def step(self, t):
        for stage, start in ((self.first_stage, 1), (self.second_stage, 3), (self.third_stage, 5), (self.line_stage, 7)):

            @pl.when((lax.rem(t, 2) == 1) & (t >= start) & (t < start + 2 * LINE))
            def _():
                stage((t - start) // 2)

    def end(self):
        last = LINE - 1
        mine = self.acc.at[last, self.b, self.y]

        @pl.when(self.a > 0)
        def _():
            self.along(last, 1).wait_recv()
            self.add(mine, self.up.at[self.a])

        @pl.when(self.a < LINE - 1)
        def _():
            self.along(last, -1).wait_recv()
            self.add(mine, self.down.at[self.a])

        self.out[...] = mine[...].astype(F32)
        for group in range(LINE):
            self.mates_sent(group)
            for k in range(3):
                self.over_y(group, k).wait_send()
                self.over_x(group, k).wait_send()
            pa = self.owner(group)

            @pl.when(pa > self.a)
            def _():
                self.along(group, 1).wait_send()

            @pl.when(pa < self.a)
            def _():
                self.along(group, -1).wait_send()


    def mates_sent(self, group):
        for pb in range(2):
            for py in range(2):
                self.to_mate(group, pb, py).wait_send()


class Place(Reduce):
    def load(self, group, pb):
        return pltpu.make_async_copy(
            self.source(group, pb, self.core), self.acc.at[group, pb, self.core], self.load_sem.at[group, pb, 0]
        )

    def source(self, group, pb, core):
        row = pl.multiple_of(((self.owner(group) * 2 + pb) * 2 + core) * self.rows, self.rows)
        return self.src.at[pl.ds(row, self.rows), :]

    def to_mate(self, group, pb, py):
        return self.remote(
            self.source(group, pb, 1 - self.core),
            self.acc.at[group, pb, py],
            self.mate_send.at[group, pb, 0],
            self.mate_recv.at[group, pb, 0],
            target(self.a, self.b, 1 - self.core, self.y),
        )

    def begin(self):
        for group in range(LINE):
            for pb in range(2):
                self.to_mate(group, pb, self.core).start()
                self.load(group, pb).start()

    def first_stage(self, group):
        for pb in range(2):
            self.load(group, pb).wait()
            self.to_mate(group, pb, 1 - self.core).wait_recv()
        for k in range(2):
            self.over_y(group, k).start()
            self.over_x(group, k).start()

    def mates_sent(self, group):
        for pb in range(2):
            self.to_mate(group, pb, self.core).wait_send()


def leave_kernel(
    back_ref,
    rows_ref,
    o_hbm,
    low_hbm,
    low_in_hbm,
    weights_hbm,
    grad_hbm,
    y_hbm,
    y_in_hbm,
    sums_ref,
    grad_ref,
    y_ref,
    o_ref,
    low_ref,
    weights_ref,
    total,
    grads,
    mate_out,
    mate_in,
    cross_out,
    cross_in,
    load_sem,
    mate_send,
    mate_recv,
    cross_send,
    cross_recv,
    *scratch,
):
    a, b, core, y = place()
    moves = core != y
    half = total.shape[0]
    wide = back_ref.shape[1]
    loads = [
        pltpu.make_async_copy(low_hbm, low_ref.at[pl.ds(0, half)], load_sem.at[0]),
        pltpu.make_async_copy(low_in_hbm, low_ref.at[pl.ds(half, half)], load_sem.at[1]),
        pltpu.make_async_copy(o_hbm, o_ref, load_sem.at[2]),
        pltpu.make_async_copy(weights_hbm.at[core], weights_ref, load_sem.at[3]),
        pltpu.make_async_copy(grad_hbm, total, load_sem.at[4]),
    ]
    for load in loads:
        load.start()
    moved = pltpu.make_async_copy(y_in_hbm, y_ref, load_sem.at[5])
    stayed = pltpu.make_async_copy(y_hbm, y_ref, load_sem.at[5])

    @pl.when(moves)
    def _():
        moved.start()

    @pl.when(jnp.logical_not(moves))
    def _():
        stayed.start()

    greet(moves)
    reduce = Place(grads, sums_ref, scratch)
    loads[3].wait()
    mate_out[...] = dot(back_ref[half:, :], weights_ref[...], NT).astype(BF16)
    exchange = reduce.remote(mate_out, mate_in, mate_send, mate_recv, target(a, b, 1 - core, y))
    exchange.start()
    loads[4].wait()
    total[...] += dot(back_ref[:half, :], weights_ref[...], NT)
    exchange.wait()
    total[...] += mate_in[...].astype(F32)
    crossing = reduce.remote(cross_out, cross_in, cross_send, cross_recv, target(a, b, y, core))

    @pl.when(moves)
    def _():
        cross_out[...] = total[...].astype(BF16)
        crossing.start()

    rows = rows_ref[...]
    for start in range(0, wide, 3 * LANES):
        span = slice(start, start + 3 * LANES)
        grads[:, span] = dot(rows, back_ref[:, span], TN).astype(BF16)
    for load in loads[:3]:
        load.wait()
    grads[:, wide:] = dot(low_ref[...], o_ref[...], TN).astype(BF16)
    reduce.begin()

    @pl.loop(1, reduce.STEPS)
    def _(t):
        reduce.step(t)

    @pl.when(moves)
    def _():
        crossing.wait()
        grad_ref[...] = cross_in[...].astype(F32)
        moved.wait()

    @pl.when(jnp.logical_not(moves))
    def _():
        grad_ref[...] = total[...]
        stayed.wait()

    reduce.end()


def leave(back, rows_all, o, low, low_in, weights, grad_one, y_own, y_in, collective_id):
    tokens, width = rows_all.shape
    half = tokens // 2
    wide, out_wide = back.shape[1], o.shape[1]
    rows = width // (4 * LINE)
    vmem, anywhere = pl.BlockSpec(memory_space=pltpu.VMEM), pl.BlockSpec(memory_space=pl.ANY)
    dma = pltpu.SemaphoreType.DMA
    return pl.pallas_call(
        leave_kernel,
        in_specs=[vmem, vmem] + [anywhere] * 7,
        out_specs=[vmem] * 3,
        out_shape=[
            jax.ShapeDtypeStruct((rows, wide + out_wide), F32),
            jax.ShapeDtypeStruct((half, width), F32),
            jax.ShapeDtypeStruct((half, width), BF16),
        ],
        scratch_shapes=[
            pltpu.VMEM((tokens, out_wide), BF16),
            pltpu.VMEM((tokens, width), BF16),
            pltpu.VMEM((width, wide), BF16),
            pltpu.VMEM((half, width), F32),
            pltpu.VMEM((width, wide + out_wide), BF16),
            pltpu.VMEM((half, width), BF16),
            pltpu.VMEM((half, width), BF16),
            pltpu.VMEM((half, width), BF16),
            pltpu.VMEM((half, width), BF16),
            dma((6,)),
            dma,
            dma,
            dma,
            dma,
            *Reduce.scratch(rows, wide + out_wide, FIRST_TILES * LANES),
        ],
        compiler_params=pltpu.CompilerParams(
            collective_id=collective_id, has_side_effects=True, vmem_limit_bytes=VMEM_BYTES
        ),
        cost_estimate=pl.CostEstimate(
            flops=4 * tokens * width * (wide + out_wide), bytes_accessed=40 * half * width, transcendentals=0
        ),
        name="leave",
    )(back, rows_all, o, low, low_in, weights, grad_one, y_own, y_in)


FF_ROWS = 256


def normalize(hidden):
    centered = hidden - jnp.mean(hidden, axis=-1, keepdims=True)
    inv_std = lax.rsqrt(jnp.mean(centered * centered, axis=-1, keepdims=True) + EPSILON)
    return centered * inv_std, inv_std


def normalize_back(grad_y, normed, inv_std, gain):
    scaled = grad_y * gain
    return inv_std * (
        scaled
        - jnp.mean(scaled, axis=-1, keepdims=True)
        - normed * jnp.mean(scaled * normed, axis=-1, keepdims=True)
    )


def feed_kernel(
    core_ref,
    x_ref,
    o_ref,
    o_in_ref,
    out_own_ref,
    out_mate_ref,
    vectors_ref,
    d_ref,
    d_in_ref,
    weights_ref,
    y_ref,
    grad_ref,
    grad_low_ref,
    do_ref,
    do_mate_ref,
    sums_ref,
    weights,
    acts,
    turned,
    factor,
    silus,
    vectors,
    totals,
    sems,
    *,
    blocks,
):
    step = pl.program_id(0)
    half_ff = weights.shape[2] // 3

    def fetch(half, kind):
        columns = pl.ds(kind * half_ff, half_ff)
        return pltpu.make_async_copy(
            weights_ref.at[half, :, columns], weights.at[half, :, columns], sems.at[half, kind]
        )

    @pl.when(step == 0)
    def _():
        for half in range(2):
            for kind in range(3):
                fetch(half, kind).start()
        vectors[...] = vectors_ref[0].astype(F32).T[:8]
        totals[...] = jnp.zeros_like(totals)

    @pl.when(step < blocks)
    def _():
        def weight(half, kind):
            return weights[half, :, kind * half_ff : (kind + 1) * half_ff]

        def ready(half, kinds):
            @pl.when(step == 0)
            def _():
                for kind in kinds:
                    fetch(half, kind).wait()

        rows = pl.ds(pl.multiple_of(step * FF_ROWS, FF_ROWS), FF_ROWS)
        gain_one, bias_one, gain_two, bias_two = (vectors[k : k + 1, :] for k in range(4))
        attn = dot(o_ref[...], out_own_ref[0], NT) + dot(o_in_ref[...], out_mate_ref[0], NT)
        first_hat, first_inv = normalize(x_ref[...].astype(F32) + attn)
        middle = first_hat * gain_one + bias_one
        middle_low = middle.astype(BF16)
        turned[0, :, rows] = middle_low.T
        mlp = middle
        for half in range(2):
            columns = slice(half * half_ff, (half + 1) * half_ff)
            ready(half, (0, 1))
            gate = dot(middle_low, weight(half, 0))
            up = dot(middle_low, weight(half, 1))
            sig = jax.nn.sigmoid(gate)
            silu = gate * sig
            hidden = (silu * up).astype(BF16)
            acts[2, rows, columns] = hidden
            silus[:, columns] = silu
            factor[:, columns] = up * sig * (1.0 + gate * (1.0 - sig))
            ready(half, (2,))
            mlp = mlp + dot(hidden, weight(half, 2), NT)
        second_hat, second_inv = normalize(mlp)
        y_ref[...] = (second_hat * gain_two + bias_two).astype(BF16)
        d = jnp.where(core_ref[1] == 1, d_in_ref[...], d_ref[...]).astype(F32)
        grad_two = normalize_back(d, second_hat, second_inv, gain_two)
        totals[2:3, :] += jnp.sum(d * second_hat, axis=0, keepdims=True)
        totals[3:4, :] += jnp.sum(d, axis=0, keepdims=True)
        grad_low = grad_two.astype(BF16)
        turned[1, :, rows] = grad_low.T
        grad_middle = grad_two
        for half in range(2):
            columns = slice(half * half_ff, (half + 1) * half_ff)
            grad_hidden = dot(grad_low, weight(half, 2))
            grad_gate = (grad_hidden * factor[:, columns]).astype(BF16)
            grad_up = (grad_hidden * silus[:, columns]).astype(BF16)
            acts[0, rows, columns] = grad_gate
            acts[1, rows, columns] = grad_up
            grad_middle = grad_middle + dot(grad_gate, weight(half, 0), NT) + dot(grad_up, weight(half, 1), NT)
        totals[0:1, :] += jnp.sum(grad_middle * first_hat, axis=0, keepdims=True)
        totals[1:2, :] += jnp.sum(grad_middle, axis=0, keepdims=True)
        grad_one = normalize_back(grad_middle, first_hat, first_inv, gain_one)
        grad_ref[...] = grad_one
        first_low = grad_one.astype(BF16)
        grad_low_ref[...] = first_low
        do_ref[...] = dot(first_low, out_own_ref[0]).astype(BF16)
        do_mate_ref[...] = dot(first_low, out_mate_ref[0]).astype(BF16)

    cut = half_ff // 2
    index = jnp.maximum(step - blocks, 0)
    half, place_in = index // 7, lax.rem(index, 7)

    @pl.when((step >= blocks) & (place_in < 6))
    def _():
        kind = place_in // 2
        start = pl.multiple_of(half * half_ff + lax.rem(place_in, 2) * cut, cut)
        sums_ref[0] = dot(turned[kind // 2], acts[kind, :, pl.ds(start, cut)]).astype(BF16)

    @pl.when((step >= blocks) & (place_in == 6))
    def _():
        sums_ref[0, :, :LANES] = totals[...].T.astype(BF16)


def feed(place_id, rows_all, o, o_in, ff_w, d_out, d_in):
    half_len, width = d_out.shape
    half_cols = o.shape[1]
    half_ff = 4 * half_cols
    blocks = half_len // FF_ROWS
    token = lambda columns: pl.BlockSpec((FF_ROWS, columns), lambda i, c: (jnp.minimum(i, blocks - 1), 0))

    def place_sums(i, c):
        k = jnp.maximum(i - blocks, 0)
        return (k // 7, 0, lax.rem(k, 7))

    return pl.pallas_call(
        functools.partial(feed_kernel, blocks=blocks),
        grid_spec=pltpu.PrefetchScalarGridSpec(
            num_scalar_prefetch=1,
            grid=(blocks + 14,),
            in_specs=[
                token(width),
                token(half_cols),
                token(half_cols),
                pl.BlockSpec((1, width, half_cols), lambda i, c: (c[0], 0, 12)),
                pl.BlockSpec((1, width, half_cols), lambda i, c: (1 - c[0], 0, 12)),
                pl.BlockSpec((1, width, LANES), lambda i, c: (0, 0, 13 * half_cols // LANES)),
                token(width),
                token(width),
                pl.BlockSpec(memory_space=pl.ANY),
            ],
            out_specs=[
                token(width),
                token(width),
                token(width),
                token(half_cols),
                token(half_cols),
                pl.BlockSpec((1, width, half_ff // 2), place_sums),
            ],
            scratch_shapes=[
                pltpu.VMEM((2, width, 3 * half_ff), BF16),
                pltpu.VMEM((3, half_len, 2 * half_ff), BF16),
                pltpu.VMEM((2, width, half_len), BF16),
                pltpu.VMEM((FF_ROWS, 2 * half_ff), F32),
                pltpu.VMEM((FF_ROWS, 2 * half_ff), F32),
                pltpu.VMEM((8, width), F32),
                pltpu.VMEM((LANES, width), F32),
                pltpu.SemaphoreType.DMA((2, 3)),
            ],
        ),
        out_shape=[
            jax.ShapeDtypeStruct((half_len, width), BF16),
            jax.ShapeDtypeStruct((half_len, width), F32),
            jax.ShapeDtypeStruct((half_len, width), BF16),
            jax.ShapeDtypeStruct((half_len, half_cols), BF16),
            jax.ShapeDtypeStruct((half_len, half_cols), BF16),
            jax.ShapeDtypeStruct((2, width, 3 * half_ff + LANES), BF16),
        ],
        compiler_params=pltpu.CompilerParams(vmem_limit_bytes=FEED_VMEM),
        cost_estimate=pl.CostEstimate(
            flops=half_len * width * (2 * 2 * width + 6 * 6 * half_ff),
            bytes_accessed=4 * ff_w.size + 20 * half_len * width,
            transcendentals=2 * half_len * half_ff,
        ),
        name="feed",
    )(place_id, rows_all, o, o_in, ff_w, ff_w, ff_w, d_out, d_in, ff_w)


def on_device(
    mp,
    devices,
    inputs,
    segments,
    w_qkv,
    w_out,
    first_gain,
    first_bias,
    w_gate,
    w_up,
    w_down,
    second_gain,
    second_bias,
    d_out,
):
    group = ("chip", "mp")
    swaps = [(a * mp + b, b * mp + a) for a in range(2) for b in range(mp) if a != b]

    core, y = lax.axis_index("core"), lax.axis_index("mp")
    moves = core != y

    def cross_in(tensor):
        return lax.ppermute(tensor, ("core", "mp"), swaps)

    def cross(tensor):
        return jnp.where(moves, cross_in(tensor), tensor)

    def mate(tensor):
        return lax.ppermute(tensor, "core", [(0, 1), (1, 0)])

    shard, half_cols = w_qkv.shape[1], w_qkv.shape[2]
    pairs = half_cols // LANES
    half_ff = w_gate.shape[1]
    half_len, width = inputs.shape
    turn = core * half_len

    attn_shard = w_qkv.reshape(3, shard, pairs, LANES).transpose(1, 2, 0, 3).reshape(shard, 3 * half_cols)
    vectors = jnp.stack([first_gain, first_bias, second_gain, second_bias], axis=1)
    pad = jnp.zeros((shard, LANES - 4), BF16)
    ff_shard = jnp.concatenate([w_gate, w_up, w_down.T, w_out.T, vectors, pad], axis=1)
    labels = cross(segments)
    attn_w, rows_all = enter(attn_shard, inputs, devices, cross, mate, 1)
    d_in = cross_in(d_out)
    after = jnp.zeros((), BF16)
    ff_w = lax.all_gather(ff_shard + after, ("mp", "chip", "core"), axis=0, tiled=True)
    ff_w = ff_w.reshape(2, width, -1)

    labels = jnp.where(core == 0, labels, jnp.roll(labels, half_len))
    cos, sin = (jnp.asarray(t) for t in rope_tables())
    place_id = jnp.stack([core, moves.astype(jnp.int32)])

    qkv = project(place_id, rows_all, attn_w, cos, sin)
    o, lse = attend(qkv, labels, turn)
    o_in = mate(o[half_len:])
    y_own, grad_one, grad_one_low, do, do_mate, ff_sum = feed(place_id, rows_all, o, o_in, ff_w, d_out, d_in)
    y_in = cross_in(y_own)
    do_in = mate(do_mate)
    grad_low_in = mate(grad_one_low)
    cos_turned, sin_turned = (
        jnp.where(core == 0, t, jnp.roll(t, half_len, axis=0)) for t in (cos, sin)
    )
    back, ff_grad = attend_back(qkv, o, do, do_in, lse, labels, cos_turned, sin_turned, ff_sum, devices, 2)
    if devices == 8 * LINE:
        attn_grad, grad_inputs, outputs = leave(
            back, rows_all, o, grad_one_low, grad_low_in, attn_w, grad_one, y_own, y_in, 3
        )
    else:
        weight_grad = dot(rows_all, back, TN).astype(BF16)
        grad_out_t = dot(jnp.concatenate([grad_one_low, grad_low_in]), o, TN).astype(BF16)
        attn_sum = jnp.concatenate([weight_grad, grad_out_t], axis=1)
        attn_sum = jnp.where(jnp.arange(2)[:, None, None] == core, attn_sum[None], 0)
        attn_grad = scatter_sum(attn_sum)
        grad_rows = dot(back, lax.dynamic_index_in_dim(attn_w, core, 0, False), NT)
        grad_rows = grad_rows[:half_len] + mate(grad_rows[half_len:].astype(BF16)).astype(F32)
        grad_inputs = grad_one + grad_rows
        grad_inputs = jnp.where(moves, cross_in(grad_inputs.astype(BF16)).astype(F32), grad_inputs)
        outputs = jnp.where(moves, y_in, y_own)

    grad_qkv = (
        attn_grad[:, : 3 * half_cols]
        .reshape(shard, pairs, 3, LANES)
        .transpose(2, 0, 1, 3)
        .reshape(3, shard, half_cols)
    )
    grad_out = attn_grad[:, 3 * half_cols :].T
    grad_gate, grad_up, grad_down_t = (ff_grad[:, k * half_ff : (k + 1) * half_ff] for k in range(3))
    grad_vectors = ff_grad[:, 3 * half_ff : 3 * half_ff + 4]
    return (
        outputs,
        grad_inputs,
        grad_qkv,
        grad_out,
        grad_vectors[:, 0],
        grad_vectors[:, 1],
        grad_gate,
        grad_up,
        grad_down_t.T,
        grad_vectors[:, 2],
        grad_vectors[:, 3],
    )


def solution(mesh):
    dp, mp = mesh.shape["dp"], mesh.shape["mp"]
    split = Mesh(mesh.devices.reshape(dp // 2, 2, mp), ("chip", "core", "mp"))
    rows = P(("chip", "core", "mp"), None)
    vector = P(("chip", "core"))
    columns = P(("chip", "core"), "mp")
    turned = P("mp", ("chip", "core"))
    stacked = P(None, ("chip", "core"), "mp")
    return jax.shard_map(
        functools.partial(on_device, mp, dp * mp),
        mesh=split,
        in_specs=(
            rows,
            vector,
            stacked,
            turned,
            vector,
            vector,
            columns,
            columns,
            turned,
            vector,
            vector,
            rows,
        ),
        out_specs=(
            rows,
            rows,
            stacked,
            turned,
            vector,
            vector,
            columns,
            columns,
            turned,
            vector,
            vector,
        ),
        check_vma=False,
    )
```

profile of v0, /device:TPU:0, one launch (start us, length us, event | category | flops | bytes accessed | tf_op | source)
XLA Modules:
  0.0 413.2 jit_solution(13333656210397186538)
XLA Ops:
  7.2 0.8 copy.49
  8.0 0.8 copy.50
  8.8 0.8 copy.51
  9.5 0.8 copy.52
  10.3 1.9 concatenate.15
  12.3 0.7 collective-permute-start
  12.9 0.8 collective-permute-start.2
  13.9 0.7 reshape.44.src
  14.6 66.8 %enter.1 = (bf16[2,768,1152]{2,1,0:T(8,128)(2,1)}, bf16[2048,768]{1,0:T(8,128)(2,1)}) custom-call(bf16[48,1152]{1,0:T(8,128)(2,1)} %reshape.44.src, bf16[1024,768]{1,0:T(8,128)(2,1)} %rows.1), custom_call_target="tpu_custom_call" | custom-call | tf_op jit(solution)/shard_map/enter/pallas_call | solution.py:636
  81.5 0.6 pad_add_fusion.core_ref
  82.1 11.8 %project.1.q_ref.k_ref.v_ref.refs_0_ = bf16[2048,1152]{1,0:T(8,128)(2,1)} custom-call(s32[2]{0:T(128)} %pad_add_fusion.core_ref, bf16[2048,768]{1,0:T(8,128)(2,1)} %get-tuple-element.26.x_ref.rows_ref, bf16[2,768,1152]{2,1,0:T(8,128)(2,1)} %get-tuple-element.27.w_ref.weights_hbm, f32[2048,128]{1,0:T(8,128)} %constant.60.clone.cos_ref, ...), custom_call_target="tpu_custom_call" | custom-call | flops 3623878656 | bytes 9633792 | tf_op jit(solution)/shard_map/project/pallas_call | solution.py:83
  93.9 0.6 compare_select_fusion
  94.5 1.4 copy.48.key_ref.refs_5_
  97.4 39.6 %attend.1 = (bf16[2048,384]{1,0:T(8,128)(2,1)}, f32[3,2,2048]{2,1,0:T(2,128)}) custom-call(s32[2]{0:T(128)} %broadcast_add_fusion.low_ref, s32[2]{0:T(128)} %get-tuple-element.49.high_ref, bf16[2048,1152]{1,0:T(8,128)(2,1)} %project.1.q_ref.k_ref.v_ref.refs_0_, bf16[2048,1152]{1,0:T(8,128)(2,1)} %project.1.q_ref.k_ref.v_ref.refs_0_, ...), custom_call_target="tpu_custom_call" | custom-call | flops 12884901888 | bytes 6291456 | tf_op jit(solution)/shard_map/attend/pallas_call | solution.py:174
  137.0 1.2 slice.63
  138.4 2.1 collective-permute-done.1.o_in_ref
  140.6 1.1 copy-done.5
  142.0 74.3 %feed.1 = (bf16[1024,768]{1,0:T(8,128)(2,1)}, f32[1024,768]{1,0:T(8,128)}, bf16[1024,768]{1,0:T(8,128)(2,1)}, bf16[1024,384]{1,0:T(8,128)(2,1)}, bf16[1024,384]{...) custom-call(s32[2]{0:T(128)} %pad_add_fusion.core_ref, bf16[2048,768]{1,0:T(8,128)(2,1)} %get-tuple-element.26.x_ref.rows_ref, ...), custom_call_target="tpu_custom_call" | custom-call | flops 45902462976 | bytes 47185920 | tf_op jit(solution)/shard_map/feed/pallas_call | solution.py:1205
  216.5 2.9 broadcast_select_fusion
  220.0 1.9 collective-permute-start.5
  221.9 0.9 copy-done.8
  222.8 110.8 %attend_back.1 = (bf16[2048,1152]{1,0:T(8,128)(2,1)}, f32[48,4736]{1,0:T(8,128)}) custom-call(bf16[2048,1152]{1,0:T(8,128)(2,1)} %project.1.q_ref.k_ref.v_ref.refs_0_, bf16[2048,384]{1,0:T(8,128)(2,1)} %get-tuple-element.28.o_ref.refs_1_.o_hbm, bf16[1024,384]{1,0:T(8,128)(2,1)} %get-tuple-element.29.refs_2_, bf16[1024,384]{1,0:T(8,128)(2,1)} %copy-done.8, ...), custom_call_target="tpu_custom_call" | custom-call | flops 32212254720 | bytes 18874368 | tf_op jit(solution)/shard_map/attend_back/pallas_call | solution.py:324
  333.6 1.7 slice_reduce_fusion
  335.2 2.1 slice_bitcast_fusion
  337.3 1.2 copy-done.7
  338.5 60.2 %leave.1 = (f32[48,1536]{1,0:T(8,128)}, f32[1024,768]{1,0:T(8,128)}, bf16[1024,768]{1,0:T(8,128)(2,1)}) custom-call(bf16[2048,1152]{1,0:T(8,128)(2,1)} %get-tuple-element.33.back_ref, bf16[2048,768]{1,0:T(8,128)(2,1)} %get-tuple-element.26.x_ref.rows_ref, bf16[2048,384]{1,0:T(8,128)(2,1)} %get-tuple-element.28.o_ref.refs_1_.o_hbm, ...), custom_call_target="tpu_custom_call" | custom-call | flops 9663676416 | bytes 31457280 | tf_op jit(solution)/shard_map/leave/pallas_call | solution.py:1022
  398.7 1.1 slice.68
  399.8 1.5 slice_bitcast_fusion.1
  401.5 0.8 reshape.48
  402.3 1.1 copy.57
  403.4 1.3 copy-done.1
  404.7 1.7 copy.58
  (41 shorter events, 3.2 us)
Async XLA Ops:
  7.2 5.1 %copy-start.4 = (s32[2048]{0:T(1024)S(1)}, s32[2048]{0:T(1024)}, u32[]{:S(2)}) copy-start(s32[2048]{0:T(1024)} %param.15) | copy-start | bytes 24580
  7.2 6.5 %copy-start.3 = (bf16[3,48,384]{2,1,0:T(8,128)(2,1)S(1)}, bf16[3,48,384]{2,1,0:T(8,128)(2,1)}, u32[]{:S(2)}) copy-start(bf16[3,48,384]{2,1,0:T(8,128)(2,1)} %param.16) | copy-start | bytes 331780
  7.2 133.4 %all-gather.2.cloned.1.call-start = ((), (), s32[]{:S(2)}) async-start(), calls=%async_computation | async-start | bytes 16220160 | tf_op jit(solution)/shard_map/all_gather | solution.py:1303
  12.3 81.6 %collective-permute-start = (s32[2048]{0:T(1024)S(1)}, s32[2048]{0:T(1024)S(1)}, u32[]{:S(2)}, u32[]{:S(2)}) collective-permute-start(s32[2048]{0:T(1024)S(1)} %copy-done.4), channel_id=1, source_target_pairs={{1,2},{2,1},{5,6},{6,5},{9,10},{10,9},{13,14},{14,13},{17,18},{18,... | collective-permute-start | bytes 24584 | tf_op jit(solution)/shard_map/ppermute | solution.py:1281
  12.9 127.6 %collective-permute-start.2 = (bf16[1024,768]{1,0:T(8,128)(2,1)}, bf16[1024,768]{1,0:T(8,128)(2,1)S(1)}, u32[]{:S(2)}, u32[]{:S(2)}) collective-permute-start(bf16[1024,768]{1,0:T(8,128)(2,1)} %d_ref.1), channel_id=1, source_target_pairs={{1,2},{2,1},{5,6},{6,5},{9,10},{10,9},{13,14},{14,13},{17,18},{18,... | collective-permute-start | bytes 4718600 | tf_op jit(solution)/shard_map/ppermute | solution.py:1281
  138.2 2.4 collective-permute-start.1
  140.6 1.4 copy-start.9
  140.6 1.2 copy-start.5
  142.0 74.5 %copy-start = (f32[2048,128]{1,0:T(8,128)S(1)}, f32[2048,128]{1,0:T(8,128)}, u32[]{:S(2)}) copy-start(f32[2048,128]{1,0:T(8,128)} %constant.60.clone.cos_ref) | copy-start | bytes 3145732
  216.3 3.7 copy-start.6
  216.3 5.6 %collective-permute-start.3 = (bf16[1024,384]{1,0:T(8,128)(2,1)}, bf16[1024,384]{1,0:T(8,128)(2,1)S(1)}, u32[]{:S(2)}, u32[]{:S(2)}) collective-permute-start(bf16[1024,384]{1,0:T(8,128)(2,1)} %get-tuple-element.30), channel_id=1, source_target_pairs={{0,2},{2,0},{1,3},{3,1},{4,6},{6,4},{5,7},{7,5},{8,10},{10,8},{9,1... | collective-permute-start | bytes 2359304 | tf_op jit(solution)/shard_map/ppermute | solution.py:1287
  219.4 117.9 %collective-permute-start.4 = (bf16[1024,768]{1,0:T(8,128)(2,1)}, bf16[1024,768]{1,0:T(8,128)(2,1)S(1)}, u32[]{:S(2)}, u32[]{:S(2)}) collective-permute-start(bf16[1024,768]{1,0:T(8,128)(2,1)} %get-tuple-element.34.low_hbm), channel_id=1, source_target_pairs={{0,2},{2,0},{1,3},{3,1},{4,6},{6,4},{5,7},{7,5},{8,10},{10,8},{9,1... | collective-permute-start | bytes 4718600 | tf_op jit(solution)/shard_map/ppermute | solution.py:1287
  220.0 117.3 %collective-permute-start.5 = (bf16[1024,768]{1,0:T(8,128)(2,1)S(1)}, bf16[1024,768]{1,0:T(8,128)(2,1)}, u32[]{:S(2)}, u32[]{:S(2)}) collective-permute-start(bf16[1024,768]{1,0:T(8,128)(2,1)S(1)} %copy-done.6), channel_id=1, source_target_pairs={{1,2},{2,1},{5,6},{6,5},{9,10},{10,9},{13,14},{14,13},{17,18},{18,... | collective-permute-start | bytes 4718600 | tf_op jit(solution)/shard_map/ppermute | solution.py:1281
  221.9 0.9 copy-start.8
  337.3 1.2 copy-start.7
  398.7 3.6 copy-start.2
  402.3 2.5 copy-start.1
Sparse Core Ops, SparseCore 0:
  12.4 118.0 all-gather.1
where the time goes:
time: 414 us; the launch traced here: 413 us
  Pallas kernels  363 us (88%)
  local copies, waits for them, and re-layouts  23.5 us (6%)
  between operations  14.2 us (3%)
  other arithmetic  5.52 us (1%)
  starting transfers between devices  4.37 us (1%)
    pallas_call x1, Pallas kernels, attend_back(): pl.pallas_call(functools.partial(attend_back_kernel, remote=remote), in_s...  111 us
    pallas_call x1, Pallas kernels, feed(): pl.pallas_call(functools.partial(feed_kernel, blocks=blocks), grid_spec=p...  74.3 us
    pallas_call x1, Pallas kernels, enter(): pl.pallas_call(enter_kernel, out_shape=[jax.ShapeDtypeStruct((2, devices...  66.8 us
    pallas_call x1, Pallas kernels, leave(): pl.pallas_call(leave_kernel, in_specs=[vmem, vmem] + [anywhere] * 7, out_...  60.2 us
    pallas_call x1, Pallas kernels, attend(): pl.pallas_call(attend_kernel, grid_spec=pltpu.PrefetchScalarGridSpec(num_...  39.6 us
    pallas_call x1, Pallas kernels, project(): pl.pallas_call(functools.partial(project_kernel, pairs=wide // (3 * LANES...  11.8 us
  transfers between devices with their start and end apart: 7, of which 1 were waited for; matrix products, arithmetic and copies ran while one was open for 3% of the time, Pallas kernels for 55%

commit v1 on v0

--- a/solution.py
+++ b/solution.py
@@ -24,7 +24,7 @@
 VMEM_BYTES = 60 << 20
 FEED_VMEM = 62 << 20
 FWD_Q, FWD_K = 1024, 512
-BWD_Q, BWD_K = 1024, 512
+BWD_K = 512
 ROW_BLOCK = 256
 MESH_ID = pl.DeviceIdType.MESH
 LINE = 4
@@ -198,24 +198,29 @@
 
 
 def attend_back_step(t, refs, scratch):
-    q_all, o_all, do_all, lse_ref, key_ref, query_ref, cos_ref, sin_ref, out_ref = refs
-    dq_turned, inner, k_turned = scratch
+    o_all, do_all, lse_ref, key_ref, query_ref, cos_ref, sin_ref, rows_ref, q_all, grads_ref = refs
+    dq_turned, inner, k_turned, held = scratch
     tokens = q_all.shape[0]
-    blocks = tokens // BWD_K
-    pair, j = t // blocks, lax.rem(t, blocks)
+    steps = 2 * tokens // BWD_K
+    pair, place_in = t // steps, lax.rem(t, steps)
+    j, h = place_in // 2, lax.rem(place_in, 2)
+    half = tokens // 2
+    turn = lax.axis_index("core") * half
     lane = lax.broadcasted_iota(jnp.int32, (1, LANES), 1)
     zero = jnp.zeros((), BF16)
-    picks = (lane < HEAD_DIM, lane >= HEAD_DIM)
+    mine = lane // HEAD_DIM == h
 
     def lanes(kind):
         return pl.ds(pl.multiple_of((pair * 3 + kind) * LANES, LANES), LANES)
 
     own = pl.ds(pl.multiple_of(pair * LANES, LANES), LANES)
-
-    def unrope(tile, rows):
-        return (tile * cos_ref[rows, :] - half_swap(tile) * sin_ref[rows, :]).astype(BF16)
-
-    @pl.when(j == 0)
+    feats = pl.ds(pl.multiple_of(h * HEAD_DIM, HEAD_DIM), HEAD_DIM)
+
+    def unrope(tile, start, rows):
+        at = pl.ds(pl.multiple_of(lax.rem(start + turn, tokens), rows), rows)
+        return (tile * cos_ref[at, :] - half_swap(tile) * sin_ref[at, :]).astype(BF16)
+
+    @pl.when(place_in == 0)
     def _():
         k_turned[...] = q_all[:, lanes(1)].T
         product = (o_all[:, own].astype(F32) * do_all[:, own].astype(F32)).T
@@ -223,66 +228,66 @@
         inner[1:2, :] = jnp.sum(product[HEAD_DIM:], axis=0, keepdims=True)
         dq_turned[...] = jnp.zeros_like(dq_turned)
 
-    key_rows = pl.ds(pl.multiple_of(j * BWD_K, BWD_K), BWD_K)
-    key_label = key_ref[key_rows, :]
-    dks, dvs = [], []
-    for h in range(2):
-        k = jnp.where(picks[h], q_all[key_rows, lanes(1)], zero)
-        v = jnp.where(picks[h], q_all[key_rows, lanes(2)], zero)
-        kt = k_turned[pl.ds(h * HEAD_DIM, HEAD_DIM), key_rows]
-
-        def body(i, carry):
-            dk, dv = carry
-            query_rows = pl.ds(pl.multiple_of(i * BWD_Q, BWD_Q), BWD_Q)
-            q = q_all[query_rows, lanes(0)]
-            do = do_all[query_rows, own]
-            s = dot(k, q, NT)
-            p = jnp.exp(s * SCALE - lse_ref[pair, pl.ds(h, 1), query_rows])
-            p = jnp.where(key_label == query_ref[:, query_rows], p, 0.0)
-            dp = dot(v, do, NT)
-            ds = (p * (dp - inner[pl.ds(h, 1), query_rows])).astype(BF16)
-            dv = dv + dot(p.astype(BF16), do)
-            dk = dk + dot(ds, q)
-            dq_turned[pl.ds(h * HEAD_DIM, HEAD_DIM), query_rows] += dot(kt, ds)
-            return dk, dv
-
-        empty = jnp.zeros((BWD_K, LANES), F32)
-        dk, dv = lax.fori_loop(0, tokens // BWD_Q, body, (empty, empty))
-        dks.append(dk)
-        dvs.append(dv)
-    out_ref[key_rows, lanes(1)] = unrope(jnp.where(picks[0], dks[0], dks[1]) * SCALE, key_rows)
-    out_ref[key_rows, lanes(2)] = jnp.where(picks[0], dvs[0], dvs[1]).astype(BF16)
-
-    @pl.when(j == blocks - 1)
-    def _():
-        out_ref[:, lanes(0)] = unrope(dq_turned[...].T * SCALE, pl.ds(0, tokens))
+    start = pl.multiple_of(j * BWD_K, BWD_K)
+    key_rows = pl.ds(start, BWD_K)
+    k = jnp.where(mine, q_all[key_rows, lanes(1)], zero)
+    v = jnp.where(mine, q_all[key_rows, lanes(2)], zero)
+    q, do = q_all[:, lanes(0)], do_all[:, own]
+    s = dot(k, q, NT)
+    p = jnp.exp(s * SCALE - lse_ref[pair, pl.ds(h, 1), :])
+    p = jnp.where(key_ref[key_rows, :] == query_ref[...], p, 0.0)
+    dp = dot(v, do, NT)
+    ds = (p * (dp - inner[pl.ds(h, 1), :])).astype(BF16)
+    dv = dot(p.astype(BF16), do)
+    dk = dot(ds, q)
+    dq_turned[feats, :] += dot(k_turned[feats, key_rows], ds)
+    results = (unrope(dk * SCALE, start, BWD_K), dv.astype(BF16))
+
+    @pl.when(h == 0)
+    def _():
+        for kind in range(2):
+            held[kind] = results[kind]
+
+    @pl.when(h == 1)
+    def _():
+        for kind in range(2):
+            q_all[key_rows, lanes(1 + kind)] = jnp.where(lane < HEAD_DIM, held[kind], results[kind])
+
+    @pl.when(place_in == steps - 1)
+    def _():
+        for at in (0, half):
+            rows = pl.ds(at, half)
+            q_all[rows, lanes(0)] = unrope(dq_turned[:, rows].T * SCALE, at, half)
+        span = pl.ds(pl.multiple_of(pair * 3 * LANES, LANES), 3 * LANES)
+        grads_ref[:, span] = dot(rows_ref[...], q_all[:, span], TN).astype(BF16)
 
 
 def attend_back_kernel(*refs, remote):
-    refs, steps = list(refs), refs[0].shape[0] // BWD_K * (refs[0].shape[1] // (3 * LANES))
-    inputs, refs = refs[:9], refs[9:]
+    refs, steps = list(refs), 2 * refs[0].shape[0] // BWD_K * (refs[0].shape[1] // (3 * LANES))
+    inputs, refs = refs[:10], refs[10:]
     do_all, do_sem, scratch = refs[-2], refs[-1], None
     refs = refs[:-2]
     half = inputs[2].shape[0]
     takes = [
         pltpu.make_async_copy(inputs[2 + k], do_all.at[pl.ds(k * half, half)], do_sem.at[k]) for k in range(2)
     ]
-    inputs = [*inputs[:2], do_all, *inputs[4:]]
+    takes.append(pltpu.make_async_copy(inputs[0], refs[1 if remote else 0], do_sem.at[2]))
+    inputs = [inputs[1], do_all, *inputs[4:]]
     for take in takes:
         take.start()
     if not remote:
-        out_ref, scratch = refs[0], refs[1:]
+        out_ref, grads_ref, scratch = refs[0], refs[1], refs[2:]
         for take in takes:
             take.wait()
 
         @pl.loop(0, steps)
         def _(t):
-            attend_back_step(t, (*inputs, out_ref), scratch)
+            attend_back_step(t, (*inputs, out_ref, grads_ref), scratch)
 
         return
-    grads, out_ref, sums, scratch = refs[0], refs[1], refs[2], refs[3:]
+    grads, out_ref, grads_ref, sums, scratch = refs[0], refs[1], refs[2], refs[3], refs[4:]
     greet(False)
-    reduce = Reduce(grads, sums, scratch[3:])
+    reduce = Reduce(grads, sums, scratch[4:])
     reduce.begin()
     for take in takes:
         take.wait()
@@ -293,25 +298,29 @@
 
         @pl.when(t < steps)
         def _():
-            attend_back_step(t, (*inputs, out_ref), scratch[:3])
+            attend_back_step(t, (*inputs, out_ref, grads_ref), scratch[:4])
 
     reduce.end()
 
 
-def attend_back(qkv, o, do, do_in, lse, labels, cos, sin, grads, devices, collective_id):
+def attend_back(qkv, o, do, do_in, lse, labels, cos, sin, rows_all, grads, devices, collective_id):
     tokens, wide = qkv.shape
     remote = devices == 8 * LINE
     queries = jnp.where(labels < 0, -2, labels)
     vmem = pl.BlockSpec(memory_space=pltpu.VMEM)
-    operands = [qkv, o, do, do_in, lse, labels[:, None], queries[None], cos, sin]
-    out_shape = [jax.ShapeDtypeStruct((tokens, wide), BF16)]
+    operands = [qkv, o, do, do_in, lse, labels[:, None], queries[None], cos, sin, rows_all]
+    out_shape = [
+        jax.ShapeDtypeStruct((tokens, wide), BF16),
+        jax.ShapeDtypeStruct((rows_all.shape[1], wide), BF16),
+    ]
     scratch = [
         pltpu.VMEM((LANES, tokens), F32),
         pltpu.VMEM((8, tokens), F32),
         pltpu.VMEM((LANES, tokens), BF16),
+        pltpu.VMEM((2, BWD_K, LANES), BF16),
     ]
     anywhere = pl.BlockSpec(memory_space=pl.ANY)
-    in_specs = [vmem, vmem, anywhere, anywhere] + [vmem] * 5
+    in_specs = [anywhere, vmem, anywhere, anywhere] + [vmem] * 6
     params = dict(vmem_limit_bytes=VMEM_BYTES)
     if remote:
         rows, width = 2 * grads.shape[1] // devices, grads.shape[2]
@@ -320,7 +329,7 @@
         out_shape.append(jax.ShapeDtypeStruct((rows, width), F32))
         scratch += Reduce.scratch(rows, width, (width // LANES + 1) // 2 * LANES)
         params.update(collective_id=collective_id, has_side_effects=True)
-    scratch += [pltpu.VMEM((tokens, wide // 3), BF16), pltpu.SemaphoreType.DMA((2,))]
+    scratch += [pltpu.VMEM((tokens, wide // 3), BF16), pltpu.SemaphoreType.DMA((3,))]
     out = pl.pallas_call(
         functools.partial(attend_back_kernel, remote=remote),
         in_specs=in_specs,
@@ -335,7 +344,7 @@
         ),
         name="attend_back",
     )(*operands)
-    return (out[0], out[1]) if remote else (out[0], scatter_sum(grads))
+    return tuple(out) if remote else (*out, scatter_sum(grads))
 
 
 def scatter_sum(grads):
@@ -380,11 +389,11 @@
 
 
 class Gather:
-    def __init__(self, src, dst, send, recv, local):
+    def __init__(self, src, dst, send, recv, local, first_tiles):
         self.src, self.dst, self.send, self.recv, self.local = src, dst, send, recv, local
         self.rows, self.width = src.shape
         tiles = self.width // LANES
-        first = FIRST_TILES * LANES if FIRST_TILES < tiles else tiles // 2 * LANES
+        first = (first_tiles or tiles // 2) * LANES
         self.columns = [(0, first), (first, self.width - first)]
         self.a, self.b, self.core, self.y = place()
 
@@ -548,12 +557,57 @@
         self.own_copy().wait()
 
 
-def enter_kernel(src, rows, dst, rows_all, copy_send, copy_recv, local, row_send, row_recv, held):
+def front_kernel(
+    attn_src,
+    rows,
+    ff_src,
+    labels_ref,
+    cos_ref,
+    sin_ref,
+    attn_w,
+    rows_all,
+    ff_w,
+    qkv_ref,
+    o_ref,
+    o_in,
+    lse_ref,
+    attn_send,
+    attn_recv,
+    attn_local,
+    ff_send,
+    ff_recv,
+    ff_local,
+    row_send,
+    row_recv,
+    label_sems,
+    o_send,
+    o_recv,
+    load_sems,
+    held,
+    labels_in,
+    query_labels,
+    key_labels,
+    weights,
+    x_ref,
+    v_turned,
+    state,
+    acc,
+):
     a, b, core, y = place()
     half = rows.shape[0]
+    tokens = 2 * half
     part = half // ROW_PARTS
     moves = core != y
+    turn = core * half
     greet(moves)
+    labels_across = pltpu.make_async_remote_copy(
+        labels_ref,
+        labels_in,
+        label_sems.at[0],
+        label_sems.at[1],
+        device_id=target(a, b, y, core),
+        device_id_type=MESH_ID,
+    )
 
     def crossing(k):
         span = pl.ds(k * part, part)
@@ -588,17 +642,22 @@
         def _():
             to_mate(rows, k).start()
 
-    @pl.when(jnp.logical_not(moves))
-    def _():
-        take.start()
-
     def hand_on(k):
         @pl.when(moves)
         def _():
             crossing(k).wait()
             to_mate(rows_all, k).start()
 
-    gather = Gather(src, dst, copy_send, copy_recv, local)
+    @pl.when(moves)
+    def _():
+        labels_across.start()
+
+    @pl.when(jnp.logical_not(moves))
+    def _():
+        take.start()
+
+    gather = Gather(attn_src, attn_w, attn_send, attn_recv, attn_local, FIRST_TILES)
+    later = Gather(ff_src, ff_w, ff_send, ff_recv, ff_local, None)
     gather.begin()
     send(0)
 
@@ -610,6 +669,7 @@
     for h in range(1, LINE):
         gather.hop(h)
         send(h)
+    later.begin()
     hand_on(0)
     hand_on(1)
     gather.turn()
@@ -624,38 +684,174 @@
     for k in range(ROW_PARTS):
         to_mate(rows_all, k).wait()
     gather.end()
-
-
-def enter(shard, rows, devices, cross, mate, collective_id):
-    shard_rows, width = shard.shape
-    if devices != 2 * 2 * 2 * LINE:
-        weights = lax.all_gather(shard, ("mp", "chip", "core"), axis=0, tiled=True)
-        own = cross(rows)
-        return weights.reshape(2, -1, width), jnp.concatenate([own, mate(own)], axis=0)
-    anywhere = pl.BlockSpec(memory_space=pl.ANY)
+    later.hop(1)
+    load_w = pltpu.make_async_copy(attn_w.at[core], weights, load_sems.at[0])
+    load_x = pltpu.make_async_copy(rows_all, x_ref, load_sems.at[1])
+    load_w.start()
+    load_x.start()
+
+    @pl.when(moves)
+    def _():
+        labels_across.wait()
+
+    labels = jnp.where(moves, labels_in[...], labels_ref[...])
+    labels = jnp.where(core == 1, jnp.concatenate([labels[:, half:], labels[:, :half]], axis=1), labels)
+    query_labels[...] = jnp.where(labels < 0, -2, labels)
+    key_labels[...] = jnp.broadcast_to(labels, (LANES, tokens)).T
+    load_w.wait()
+    load_x.wait()
+    pairs = weights.shape[1] // (3 * LANES)
+
+    @pl.loop(0, tokens // ROW_BLOCK)
+    def _(i):
+        at = pl.ds(pl.multiple_of(i * ROW_BLOCK, ROW_BLOCK), ROW_BLOCK)
+        table = pl.ds(pl.multiple_of(lax.rem(i * ROW_BLOCK + turn, tokens), ROW_BLOCK), ROW_BLOCK)
+        x = x_ref[at, :]
+        cos, sin = cos_ref[table, :], sin_ref[table, :]
+        for pair in range(pairs):
+            base = pair * 3 * LANES
+            tile = dot(x, weights[:, base : base + 3 * LANES])
+            for kind in range(2):
+                span = slice(base + kind * LANES, base + (kind + 1) * LANES)
+                flat = tile[:, kind * LANES : (kind + 1) * LANES]
+                qkv_ref[at, span] = (flat * cos + half_swap(flat) * sin).astype(BF16)
+            qkv_ref[at, base + 2 * LANES : base + 3 * LANES] = tile[:, 2 * LANES :].astype(BF16)
+
+    later.hop(2)
+    lane = lax.broadcasted_iota(jnp.int32, (1, LANES), 1)
+    zero = jnp.zeros((), BF16)
+    blocks = tokens // FWD_K
+
+    def o_to_mate(pair):
+        span = pl.ds(pl.multiple_of(pair * LANES, LANES), LANES)
+        return pltpu.make_async_remote_copy(
+            o_ref.at[pl.ds(half, half), span],
+            o_in.at[:, span],
+            o_send.at[pair],
+            o_recv.at[pair],
+            device_id=target(a, b, 1 - core, y),
+            device_id_type=MESH_ID,
+        )
+
+    @pl.loop(0, pairs * blocks)
+    def _(t):
+        pair, j = t // blocks, lax.rem(t, blocks)
+
+        def lanes(kind):
+            return pl.ds(pl.multiple_of((pair * 3 + kind) * LANES, LANES), LANES)
+
+        @pl.when(t == blocks)
+        def _():
+            later.hop(3)
+
+        @pl.when(t == 2 * blocks)
+        def _():
+            later.turn()
+
+        @pl.when(j == 0)
+        def _():
+            v_turned[...] = qkv_ref[:, lanes(2)].T
+            for h in range(2):
+                state[2 * h : 2 * h + 1, :] = jnp.full((1, tokens), MASKED, F32)
+                state[2 * h + 1 : 2 * h + 2, :] = jnp.zeros((1, tokens), F32)
+            acc[...] = jnp.zeros_like(acc)
+
+        keys = pl.ds(pl.multiple_of(j * FWD_K, FWD_K), FWD_K)
+        k = qkv_ref[keys, lanes(1)]
+        q = qkv_ref[:, lanes(0)] * jnp.asarray(SCALE, BF16)
+        same = key_labels[keys, :1] == query_labels[...]
+        for h in range(2):
+            feats = slice(h * HEAD_DIM, (h + 1) * HEAD_DIM)
+            s = dot(k, jnp.where(lane // HEAD_DIM == h, q, zero), NT)
+            s = jnp.where(same, s, -1e30)
+            top, total = state[2 * h : 2 * h + 1, :], state[2 * h + 1 : 2 * h + 2, :]
+            new_top = jnp.maximum(top, jnp.max(s, axis=0, keepdims=True))
+            fade = jnp.exp(top - new_top)
+            e = jnp.exp(s - new_top)
+            state[2 * h : 2 * h + 1, :] = new_top
+            state[2 * h + 1 : 2 * h + 2, :] = fade * total + jnp.sum(e, axis=0, keepdims=True)
+            acc[feats, :] = acc[feats, :] * fade + dot(v_turned[feats, keys], e.astype(BF16))
+
+        @pl.when(j == blocks - 1)
+        def _():
+            for h in range(2):
+                feats = slice(h * HEAD_DIM, (h + 1) * HEAD_DIM)
+                norm = jnp.maximum(state[2 * h + 1 : 2 * h + 2, :], 1.0)
+                acc[feats, :] = acc[feats, :] / norm
+                lse_ref[pair, pl.ds(h, 1), :] = state[2 * h : 2 * h + 1, :] + jnp.log(norm)
+            o_ref[:, pl.ds(pl.multiple_of(pair * LANES, LANES), LANES)] = acc[...].T.astype(BF16)
+            o_to_mate(pair).start()
+
+    later.last()
+    later.end()
+    for pair in range(pairs):
+        o_to_mate(pair).wait()
+
+
+def front(attn_shard, rows, ff_shard, segments, cos, sin, devices, collective_id):
+    shard, wide = attn_shard.shape
+    half, width = rows.shape
+    tokens, out_wide = 2 * half, wide // 3
+    vmem, anywhere = pl.BlockSpec(memory_space=pltpu.VMEM), pl.BlockSpec(memory_space=pl.ANY)
+    dma = pltpu.SemaphoreType.DMA
     return pl.pallas_call(
-        enter_kernel,
+        front_kernel,
+        in_specs=[anywhere, anywhere, anywhere, vmem, vmem, vmem],
+        out_specs=[anywhere, anywhere, anywhere, vmem, vmem, anywhere, vmem],
         out_shape=[
-            jax.ShapeDtypeStruct((2, devices // 2 * shard_rows, width), shard.dtype),
-            jax.ShapeDtypeStruct((2 * rows.shape[0], rows.shape[1]), rows.dtype),
+            jax.ShapeDtypeStruct((2, devices // 2 * shard, wide), BF16),
+            jax.ShapeDtypeStruct((tokens, width), BF16),
+            jax.ShapeDtypeStruct((2, devices // 2 * shard, ff_shard.shape[1]), BF16),
+            jax.ShapeDtypeStruct((tokens, wide), BF16),
+            jax.ShapeDtypeStruct((tokens, out_wide), BF16),
+            jax.ShapeDtypeStruct((half, out_wide), BF16),
+            jax.ShapeDtypeStruct((out_wide // LANES, 2, tokens), F32),
         ],
-        in_specs=[anywhere, anywhere],
-        out_specs=[anywhere, anywhere],
         scratch_shapes=[
-            pltpu.SemaphoreType.DMA((62,)),
-            pltpu.SemaphoreType.DMA((62,)),
-            pltpu.SemaphoreType.DMA,
-            pltpu.SemaphoreType.DMA((2, ROW_PARTS)),
-            pltpu.SemaphoreType.DMA((3, ROW_PARTS)),
-            pltpu.VMEM(rows.shape, rows.dtype),
+            dma((62,)),
+            dma((62,)),
+            dma,
+            dma((62,)),
+            dma((62,)),
+            dma,
+            dma((2, ROW_PARTS)),
+            dma((3, ROW_PARTS)),
+            dma((2,)),
+            dma((out_wide // LANES,)),
+            dma((out_wide // LANES,)),
+            dma((2,)),
+            pltpu.VMEM((half, width), BF16),
+            pltpu.VMEM((1, tokens), jnp.int32),
+            pltpu.VMEM((1, tokens), jnp.int32),
+            pltpu.VMEM((tokens, LANES), jnp.int32),
+            pltpu.VMEM((width, wide), BF16),
+            pltpu.VMEM((tokens, width), BF16),
+            pltpu.VMEM((LANES, tokens), BF16),
+            pltpu.VMEM((8, tokens), F32),
+            pltpu.VMEM((LANES, tokens), F32),
         ],
-        compiler_params=pltpu.CompilerParams(collective_id=collective_id, has_side_effects=True),
-        name="enter",
-    )(shard, rows)
+        compiler_params=pltpu.CompilerParams(
+            collective_id=collective_id, has_side_effects=True, vmem_limit_bytes=VMEM_BYTES
+        ),
+        cost_estimate=pl.CostEstimate(
+            flops=2 * tokens * width * wide + 8 * tokens * tokens * out_wide,
+            bytes_accessed=40 * half * width,
+            transcendentals=2 * out_wide // LANES * tokens * tokens,
+        ),
+        name="front",
+    )(attn_shard, rows, ff_shard, segments.reshape(1, tokens), cos, sin)
+
+
+def enter(shard, rows, cross, mate):
+    weights = lax.all_gather(shard, ("mp", "chip", "core"), axis=0, tiled=True)
+    own = cross(rows)
+    return weights.reshape(2, -1, shard.shape[1]), jnp.concatenate([own, mate(own)], axis=0)
 
 
 class Reduce:
-    STEPS = 14
+    SPACING = 4
+    OFFSETS = (1, 5, 9, 13)
+    STEPS = OFFSETS[-1] + SPACING * (LINE - 1) + 1
 
     def __init__(self, src, out, scratch):
         self.src, self.out = src, out
@@ -834,11 +1030,13 @@
             self.along(group, -1).start()
 
     def step(self, t):
-        for stage, start in ((self.first_stage, 1), (self.second_stage, 3), (self.third_stage, 5), (self.line_stage, 7)):
-
-            @pl.when((lax.rem(t, 2) == 1) & (t >= start) & (t < start + 2 * LINE))
+        stages = (self.first_stage, self.second_stage, self.third_stage, self.line_stage)
+        for stage, start in zip(stages, self.OFFSETS):
+            passed = t - start
+
+            @pl.when((passed >= 0) & (passed < self.SPACING * LINE) & (lax.rem(passed, self.SPACING) == 0))
             def _():
-                stage((t - start) // 2)
+                stage(passed // self.SPACING)
 
     def end(self):
         last = LINE - 1
@@ -878,6 +1076,10 @@
 
 
 class Place(Reduce):
+    SPACING = 1
+    OFFSETS = (0, 1, 2, 3)
+    STEPS = OFFSETS[-1] + SPACING * (LINE - 1) + 1
+
     def load(self, group, pb):
         return pltpu.make_async_copy(
             self.source(group, pb, self.core), self.acc.at[group, pb, self.core], self.load_sem.at[group, pb, 0]
@@ -917,17 +1119,14 @@
 
 def leave_kernel(
     back_ref,
-    rows_ref,
+    done_hbm,
     o_hbm,
     low_hbm,
     low_in_hbm,
     weights_hbm,
     grad_hbm,
-    y_hbm,
-    y_in_hbm,
     sums_ref,
     grad_ref,
-    y_ref,
     o_ref,
     low_ref,
     weights_ref,
@@ -949,6 +1148,7 @@
     half = total.shape[0]
     wide = back_ref.shape[1]
     loads = [
+        pltpu.make_async_copy(done_hbm, grads.at[:, pl.ds(0, wide)], load_sem.at[6]),
         pltpu.make_async_copy(low_hbm, low_ref.at[pl.ds(0, half)], load_sem.at[0]),
         pltpu.make_async_copy(low_in_hbm, low_ref.at[pl.ds(half, half)], load_sem.at[1]),
         pltpu.make_async_copy(o_hbm, o_ref, load_sem.at[2]),
@@ -957,63 +1157,55 @@
     ]
     for load in loads:
         load.start()
-    moved = pltpu.make_async_copy(y_in_hbm, y_ref, load_sem.at[5])
-    stayed = pltpu.make_async_copy(y_hbm, y_ref, load_sem.at[5])
-
-    @pl.when(moves)
-    def _():
-        moved.start()
-
-    @pl.when(jnp.logical_not(moves))
-    def _():
-        stayed.start()
-
     greet(moves)
     reduce = Place(grads, sums_ref, scratch)
-    loads[3].wait()
+    for load in loads[:4]:
+        load.wait()
+    grads[:, wide:] = dot(low_ref[...], o_ref[...], TN).astype(BF16)
+    reduce.begin()
+    loads[4].wait()
     mate_out[...] = dot(back_ref[half:, :], weights_ref[...], NT).astype(BF16)
     exchange = reduce.remote(mate_out, mate_in, mate_send, mate_recv, target(a, b, 1 - core, y))
     exchange.start()
-    loads[4].wait()
+    loads[5].wait()
     total[...] += dot(back_ref[:half, :], weights_ref[...], NT)
     exchange.wait()
     total[...] += mate_in[...].astype(F32)
-    crossing = reduce.remote(cross_out, cross_in, cross_send, cross_recv, target(a, b, y, core))
+    part = half // LINE
+
+    def crossing(k):
+        span = pl.ds(pl.multiple_of(k * part, part), part)
+        return reduce.remote(
+            cross_out.at[span], cross_in.at[span], cross_send.at[k], cross_recv.at[k], target(a, b, y, core)
+        )
 
     @pl.when(moves)
     def _():
         cross_out[...] = total[...].astype(BF16)
-        crossing.start()
-
-    rows = rows_ref[...]
-    for start in range(0, wide, 3 * LANES):
-        span = slice(start, start + 3 * LANES)
-        grads[:, span] = dot(rows, back_ref[:, span], TN).astype(BF16)
-    for load in loads[:3]:
-        load.wait()
-    grads[:, wide:] = dot(low_ref[...], o_ref[...], TN).astype(BF16)
-    reduce.begin()
-
-    @pl.loop(1, reduce.STEPS)
+
+    @pl.loop(0, reduce.STEPS)
     def _(t):
         reduce.step(t)
 
+        @pl.when(moves & (t >= 1) & (t <= LINE))
+        def _():
+            crossing(t - 1).start()
+
     @pl.when(moves)
     def _():
-        crossing.wait()
+        for k in range(LINE):
+            crossing(k).wait()
         grad_ref[...] = cross_in[...].astype(F32)
-        moved.wait()
 
     @pl.when(jnp.logical_not(moves))
     def _():
         grad_ref[...] = total[...]
-        stayed.wait()
 
     reduce.end()
 
 
-def leave(back, rows_all, o, low, low_in, weights, grad_one, y_own, y_in, collective_id):
-    tokens, width = rows_all.shape
+def leave(back, done, o, low, low_in, weights, grad_one, collective_id):
+    tokens, width = back.shape[0], grad_one.shape[1]
     half = tokens // 2
     wide, out_wide = back.shape[1], o.shape[1]
     rows = width // (4 * LINE)
@@ -1021,12 +1213,11 @@
     dma = pltpu.SemaphoreType.DMA
     return pl.pallas_call(
         leave_kernel,
-        in_specs=[vmem, vmem] + [anywhere] * 7,
-        out_specs=[vmem] * 3,
+        in_specs=[vmem] + [anywhere] * 6,
+        out_specs=[vmem] * 2,
         out_shape=[
             jax.ShapeDtypeStruct((rows, wide + out_wide), F32),
             jax.ShapeDtypeStruct((half, width), F32),
-            jax.ShapeDtypeStruct((half, width), BF16),
         ],
         scratch_shapes=[
             pltpu.VMEM((tokens, out_wide), BF16),
@@ -1038,11 +1229,11 @@
             pltpu.VMEM((half, width), BF16),
             pltpu.VMEM((half, width), BF16),
             pltpu.VMEM((half, width), BF16),
-            dma((6,)),
+            dma((7,)),
             dma,
             dma,
-            dma,
-            dma,
+            dma((LINE,)),
+            dma((LINE,)),
             *Reduce.scratch(rows, wide + out_wide, FIRST_TILES * LANES),
         ],
         compiler_params=pltpu.CompilerParams(
@@ -1052,7 +1243,7 @@
             flops=4 * tokens * width * (wide + out_wide), bytes_accessed=40 * half * width, transcendentals=0
         ),
         name="leave",
-    )(back, rows_all, o, low, low_in, weights, grad_one, y_own, y_in)
+    )(back, done, o, low, low_in, weights, grad_one)
 
 
 FF_ROWS = 256
@@ -1074,12 +1265,10 @@
 
 
 def feed_kernel(
-    core_ref,
     x_ref,
     o_ref,
     o_in_ref,
-    out_own_ref,
-    out_mate_ref,
+    out_ref,
     vectors_ref,
     d_ref,
     d_in_ref,
@@ -1098,10 +1287,53 @@
     vectors,
     totals,
     sems,
+    y_slots,
+    y_send,
+    y_recv,
     *,
     blocks,
+    remote,
 ):
     step = pl.program_id(0)
+    a, b, core, y = place()
+    moves = core != y
+
+    def at_home(k):
+        span = pl.ds(pl.multiple_of(k * FF_ROWS, FF_ROWS), FF_ROWS)
+        return pltpu.make_async_copy(y_slots.at[lax.rem(k, 2)], y_ref.at[span], y_send.at[lax.rem(k, 2)])
+
+    def across(k):
+        span = pl.ds(pl.multiple_of(k * FF_ROWS, FF_ROWS), FF_ROWS)
+        return pltpu.make_async_remote_copy(
+            y_slots.at[lax.rem(k, 2)],
+            y_ref.at[span],
+            y_send.at[lax.rem(k, 2)],
+            y_recv.at[k],
+            device_id=target(a, b, y, core),
+            device_id_type=MESH_ID,
+        )
+
+    def each(k, move, stay):
+        if remote:
+
+            @pl.when(moves)
+            def _():
+                move(across(k))
+
+            @pl.when(jnp.logical_not(moves))
+            def _():
+                stay(at_home(k))
+        else:
+            stay(at_home(k))
+
+    if remote:
+
+        @pl.when((step == 0) & moves)
+        def _():
+            barrier = pltpu.get_barrier_semaphore()
+            pl.semaphore_signal(barrier, inc=1, device_id=target(a, b, y, core), device_id_type=MESH_ID)
+            pl.semaphore_wait(barrier, 1)
+
     half_ff = weights.shape[2] // 3
 
     def fetch(half, kind):
@@ -1131,7 +1363,7 @@
 
         rows = pl.ds(pl.multiple_of(step * FF_ROWS, FF_ROWS), FF_ROWS)
         gain_one, bias_one, gain_two, bias_two = (vectors[k : k + 1, :] for k in range(4))
-        attn = dot(o_ref[...], out_own_ref[0], NT) + dot(o_in_ref[...], out_mate_ref[0], NT)
+        attn = dot(o_ref[...], out_ref[core], NT) + dot(o_in_ref[...], out_ref[1 - core], NT)
         first_hat, first_inv = normalize(x_ref[...].astype(F32) + attn)
         middle = first_hat * gain_one + bias_one
         middle_low = middle.astype(BF16)
@@ -1151,8 +1383,14 @@
             ready(half, (2,))
             mlp = mlp + dot(hidden, weight(half, 2), NT)
         second_hat, second_inv = normalize(mlp)
-        y_ref[...] = (second_hat * gain_two + bias_two).astype(BF16)
-        d = jnp.where(core_ref[1] == 1, d_in_ref[...], d_ref[...]).astype(F32)
+
+        @pl.when(step >= 2)
+        def _():
+            each(step - 2, lambda copy: copy.wait_send(), lambda copy: copy.wait())
+
+        y_slots[lax.rem(step, 2)] = (second_hat * gain_two + bias_two).astype(BF16)
+        each(step, lambda copy: copy.start(), lambda copy: copy.start())
+        d = jnp.where(moves, d_in_ref[...], d_ref[...]).astype(F32)
         grad_two = normalize_back(d, second_hat, second_inv, gain_two)
         totals[2:3, :] += jnp.sum(d * second_hat, axis=0, keepdims=True)
         totals[3:4, :] += jnp.sum(d, axis=0, keepdims=True)
@@ -1173,8 +1411,19 @@
         grad_ref[...] = grad_one
         first_low = grad_one.astype(BF16)
         grad_low_ref[...] = first_low
-        do_ref[...] = dot(first_low, out_own_ref[0]).astype(BF16)
-        do_mate_ref[...] = dot(first_low, out_mate_ref[0]).astype(BF16)
+        do_ref[...] = dot(first_low, out_ref[core]).astype(BF16)
+        do_mate_ref[...] = dot(first_low, out_ref[1 - core]).astype(BF16)
+
+    @pl.when(step == blocks + 13)
+    def _():
+        for k in (blocks - 2, blocks - 1):
+            each(jnp.int32(k), lambda copy: copy.wait_send(), lambda copy: copy.wait())
+        if remote:
+
+            @pl.when(moves)
+            def _():
+                for k in range(blocks):
+                    across(jnp.int32(k)).wait_recv()
 
     cut = half_ff // 2
     index = jnp.maximum(step - blocks, 0)
@@ -1191,35 +1440,38 @@
         sums_ref[0, :, :LANES] = totals[...].T.astype(BF16)
 
 
-def feed(place_id, rows_all, o, o_in, ff_w, d_out, d_in):
+def feed(rows_all, o, o_in, ff_w, d_out, d_in, devices, collective_id):
     half_len, width = d_out.shape
     half_cols = o.shape[1]
     half_ff = 4 * half_cols
     blocks = half_len // FF_ROWS
-    token = lambda columns: pl.BlockSpec((FF_ROWS, columns), lambda i, c: (jnp.minimum(i, blocks - 1), 0))
-
-    def place_sums(i, c):
+    token = lambda columns: pl.BlockSpec((FF_ROWS, columns), lambda i: (jnp.minimum(i, blocks - 1), 0))
+
+    params = dict(vmem_limit_bytes=FEED_VMEM)
+    if devices == 8 * LINE:
+        params.update(collective_id=collective_id, has_side_effects=True)
+
+    def place_sums(i):
         k = jnp.maximum(i - blocks, 0)
         return (k // 7, 0, lax.rem(k, 7))
 
     return pl.pallas_call(
-        functools.partial(feed_kernel, blocks=blocks),
+        functools.partial(feed_kernel, blocks=blocks, remote=devices == 8 * LINE),
         grid_spec=pltpu.PrefetchScalarGridSpec(
-            num_scalar_prefetch=1,
+            num_scalar_prefetch=0,
             grid=(blocks + 14,),
             in_specs=[
                 token(width),
                 token(half_cols),
                 token(half_cols),
-                pl.BlockSpec((1, width, half_cols), lambda i, c: (c[0], 0, 12)),
-                pl.BlockSpec((1, width, half_cols), lambda i, c: (1 - c[0], 0, 12)),
-                pl.BlockSpec((1, width, LANES), lambda i, c: (0, 0, 13 * half_cols // LANES)),
+                pl.BlockSpec((2, width, half_cols), lambda i: (0, 0, 12)),
+                pl.BlockSpec((1, width, LANES), lambda i: (0, 0, 13 * half_cols // LANES)),
                 token(width),
                 token(width),
                 pl.BlockSpec(memory_space=pl.ANY),
             ],
             out_specs=[
-                token(width),
+                pl.BlockSpec(memory_space=pl.ANY),
                 token(width),
                 token(width),
                 token(half_cols),
@@ -1235,6 +1487,9 @@
                 pltpu.VMEM((8, width), F32),
                 pltpu.VMEM((LANES, width), F32),
                 pltpu.SemaphoreType.DMA((2, 3)),
+                pltpu.VMEM((2, FF_ROWS, width), BF16),
+                pltpu.SemaphoreType.DMA((2,)),
+                pltpu.SemaphoreType.DMA((blocks,)),
             ],
         ),
         out_shape=[
@@ -1245,14 +1500,14 @@
             jax.ShapeDtypeStruct((half_len, half_cols), BF16),
             jax.ShapeDtypeStruct((2, width, 3 * half_ff + LANES), BF16),
         ],
-        compiler_params=pltpu.CompilerParams(vmem_limit_bytes=FEED_VMEM),
+        compiler_params=pltpu.CompilerParams(**params),
         cost_estimate=pl.CostEstimate(
             flops=half_len * width * (2 * 2 * width + 6 * 6 * half_ff),
             bytes_accessed=4 * ff_w.size + 20 * half_len * width,
             transcendentals=2 * half_len * half_ff,
         ),
         name="feed",
-    )(place_id, rows_all, o, o_in, ff_w, ff_w, ff_w, d_out, d_in, ff_w)
+    )(rows_all, o, o_in, ff_w, ff_w, d_out, d_in, ff_w)
 
 
 def on_device(
@@ -1297,33 +1552,31 @@
     pad = jnp.zeros((shard, LANES - 4), BF16)
     ff_shard = jnp.concatenate([w_gate, w_up, w_down.T, w_out.T, vectors, pad], axis=1)
     labels = cross(segments)
-    attn_w, rows_all = enter(attn_shard, inputs, devices, cross, mate, 1)
+    labels = jnp.where(core == 0, labels, jnp.roll(labels, half_len))
     d_in = cross_in(d_out)
-    after = jnp.zeros((), BF16)
-    ff_w = lax.all_gather(ff_shard + after, ("mp", "chip", "core"), axis=0, tiled=True)
-    ff_w = ff_w.reshape(2, width, -1)
-
-    labels = jnp.where(core == 0, labels, jnp.roll(labels, half_len))
     cos, sin = (jnp.asarray(t) for t in rope_tables())
     place_id = jnp.stack([core, moves.astype(jnp.int32)])
-
-    qkv = project(place_id, rows_all, attn_w, cos, sin)
-    o, lse = attend(qkv, labels, turn)
-    o_in = mate(o[half_len:])
-    y_own, grad_one, grad_one_low, do, do_mate, ff_sum = feed(place_id, rows_all, o, o_in, ff_w, d_out, d_in)
-    y_in = cross_in(y_own)
+    if devices == 8 * LINE:
+        attn_w, rows_all, ff_w, qkv, o, o_in, lse = front(
+            attn_shard, inputs, ff_shard, segments, cos, sin, devices, 1
+        )
+    else:
+        attn_w, rows_all = enter(attn_shard, inputs, cross, mate)
+        ff_w = lax.all_gather(ff_shard, ("mp", "chip", "core"), axis=0, tiled=True).reshape(2, width, -1)
+        qkv = project(place_id, rows_all, attn_w, cos, sin)
+        o, lse = attend(qkv, labels, turn)
+        o_in = mate(o[half_len:])
+    outputs, grad_one, grad_one_low, do, do_mate, ff_sum = feed(rows_all, o, o_in, ff_w, d_out, d_in, devices, 4)
     do_in = mate(do_mate)
     grad_low_in = mate(grad_one_low)
-    cos_turned, sin_turned = (
-        jnp.where(core == 0, t, jnp.roll(t, half_len, axis=0)) for t in (cos, sin)
+    back, weight_grad, ff_grad = attend_back(
+        qkv, o, do, do_in, lse, labels, cos, sin, rows_all, ff_sum, devices, 2
     )
-    back, ff_grad = attend_back(qkv, o, do, do_in, lse, labels, cos_turned, sin_turned, ff_sum, devices, 2)
     if devices == 8 * LINE:
-        attn_grad, grad_inputs, outputs = leave(
-            back, rows_all, o, grad_one_low, grad_low_in, attn_w, grad_one, y_own, y_in, 3
+        attn_grad, grad_inputs = leave(
+            back, weight_grad, o, grad_one_low, grad_low_in, attn_w, grad_one, 3
         )
     else:
-        weight_grad = dot(rows_all, back, TN).astype(BF16)
         grad_out_t = dot(jnp.concatenate([grad_one_low, grad_low_in]), o, TN).astype(BF16)
         attn_sum = jnp.concatenate([weight_grad, grad_out_t], axis=1)
         attn_sum = jnp.where(jnp.arange(2)[:, None, None] == core, attn_sum[None], 0)
@@ -1332,7 +1585,7 @@
         grad_rows = grad_rows[:half_len] + mate(grad_rows[half_len:].astype(BF16)).astype(F32)
         grad_inputs = grad_one + grad_rows
         grad_inputs = jnp.where(moves, cross_in(grad_inputs.astype(BF16)).astype(F32), grad_inputs)
-        outputs = jnp.where(moves, y_in, y_own)
+        outputs = cross(outputs)
 
     grad_qkv = (
         attn_grad[:, : 3 * half_cols]

time: 414 us -> 400 us (0.966)
  between operations: 14.2 us -> 0.77 us
  other arithmetic: 5.52 us -> 0.61 us
    pallas_call x1, Pallas kernels: 111 us -> 98.1 us  [attend_back(): pl.pallas_call(functools.partial(attend_back_kernel, remote=remote), in_s...]
    pallas_call x5 -> x3, Pallas kernels: 253 us -> 263 us  [the longest x1 136 us: front(): pl.pallas_call(front_kernel, in_specs=[anywhere, anywhere, anywhere, vmem...]
    ppermute x3 -> x2, starting transfers between devices: 1.02 us -> 5.31 us  [mate(): return lax.ppermute(tensor, 'core', [(0, 1), (1, 0)])]
  transfers between devices with their start and end apart: 7 -> 4, of which waited for: 1 -> 0; matrix products, arithmetic and copies ran while one was open for 3% -> 3% of each run, Pallas kernels for 55% -> 59%
where the time goes in v1:
time: 400 us; the launch traced here: 396 us
  Pallas kernels  361 us (90%)
  local copies, waits for them, and re-layouts  26.2 us (7%)
  starting transfers between devices  6.72 us (2%)
    pallas_call x1, Pallas kernels, front(): pl.pallas_call(front_kernel, in_specs=[anywhere, anywhere, anywhere, vmem...  136 us
    pallas_call x1, Pallas kernels, attend_back(): pl.pallas_call(functools.partial(attend_back_kernel, remote=remote), in_s...  98.1 us
    pallas_call x1, Pallas kernels, feed(): pl.pallas_call(functools.partial(feed_kernel, blocks=blocks, remote=devic...  74.1 us
    pallas_call x1, Pallas kernels, leave(): pl.pallas_call(leave_kernel, in_specs=[vmem] + [anywhere] * 6, out_specs=...  53.1 us
  transfers between devices with their start and end apart: 4, of which 0 were waited for; matrix products, arithmetic and copies ran while one was open for 3% of the time, Pallas kernels for 59%

profile of v1, /device:TPU:0, one launch (start us, length us, event | category | flops | bytes accessed | tf_op | source)
XLA Modules:
  0.0 395.6 jit_solution(10303718585637351362)
XLA Ops:
  0.6 0.8 collective-permute-start
  1.4 0.8 copy.32
  2.2 0.8 copy.33
  2.9 0.8 copy.34
  3.7 0.8 copy.35
  4.4 0.9 reshape.37
  5.4 0.1 copy.31
  5.5 0.7 reshape.38.attn_src
  6.2 1.9 concatenate.7.ff_src
  8.2 136.0 %front.1 = (bf16[2,768,1152]{2,1,0:T(8,128)(2,1)}, bf16[2048,768]{1,0:T(8,128)(2,1)}, bf16[2,768,5120]{2,1,0:T(8,128)(2,1)}, bf16[2048,1152]{1,0:T(8,128)(2,1)},...) custom-call(bf16[48,1152]{1,0:T(8,128)(2,1)} %reshape.38.attn_src, ...), custom_call_target="tpu_custom_call" | custom-call | flops 16508780544 | bytes 31457280 | tf_op jit(solution)/shard_map/front/pallas_call | solution.py:797
  144.2 0.0 copy-start.3
  144.2 1.1 copy-done.3
  145.4 74.1 %feed.1 = (bf16[1024,768]{1,0:T(8,128)(2,1)}, f32[1024,768]{1,0:T(8,128)}, bf16[1024,768]{1,0:T(8,128)(2,1)}, bf16[1024,384]{1,0:T(8,128)(2,1)}, bf16[1024,384]{...) custom-call(bf16[2048,768]{1,0:T(8,128)(2,1)} %get-tuple-element.29.x_ref.refs_9_, ...), custom_call_target="tpu_custom_call" | custom-call | flops 45902462976 | bytes 47185920 | tf_op jit(solution)/shard_map/feed/pallas_call | solution.py:1458
  219.5 1.0 collective-permute-start.1
  220.5 0.7 collective-permute-start.2
  221.2 0.0 collective-permute-done.2
  221.2 0.6 compare_select_fusion
  221.8 1.3 copy.36.refs_5_
  223.2 4.3 %collective-permute-start.3 = (bf16[1024,768]{1,0:T(8,128)(2,1)}, bf16[1024,768]{1,0:T(8,128)(2,1)S(1)}, u32[]{:S(2)}, u32[]{:S(2)}) collective-permute-start(bf16[1024,768]{1,0:T(8,128)(2,1)} %get-tuple-element.41.low_hbm), channel_id=1, source_target_pairs={{0,2},{2,0},{1,3},{3,1},{4,6},{6,4},{5,7},{7,5},{8,10},{10,8},{9,1... | collective-permute-start | bytes 4718600 | tf_op jit(solution)/shard_map/ppermute | solution.py:1542
  227.5 0.9 copy-done.4
  228.4 98.1 %attend_back.1 = (bf16[2048,1152]{1,0:T(8,128)(2,1)}, bf16[768,1152]{1,0:T(8,128)(2,1)}, f32[48,4736]{1,0:T(8,128)}) custom-call(bf16[2048,1152]{1,0:T(8,128)(2,1)} %get-tuple-element.34.refs_0_, bf16[2048,384]{1,0:T(8,128)(2,1)} %get-tuple-element.30.o_ref.refs_1_.o_hbm, bf16[1024,384]{1,0:T(8,128)(2,1)} %get-tuple-element.35.refs_2_, ...), custom_call_target="tpu_custom_call" | custom-call | flops 32212254720 | bytes 18874368 | tf_op jit(solution)/shard_map/attend_back/pallas_call | solution.py:333
  326.5 1.6 slice_reduce_fusion
  328.1 2.1 slice_bitcast_fusion
  330.2 1.1 copy-done.2
  331.3 53.1 %leave.1 = (f32[48,1536]{1,0:T(8,128)}, f32[1024,768]{1,0:T(8,128)}) custom-call(bf16[2048,1152]{1,0:T(8,128)(2,1)} %get-tuple-element.39.back_ref, bf16[768,1152]{1,0:T(8,128)(2,1)} %get-tuple-element.40.done_hbm, bf16[2048,384]{1,0:T(8,128)(2,1)} %get-tuple-element.30.o_ref.refs_1_.o_hbm, bf16[1024,768]{1,0:T(8,128)(2,1)} %get-tuple-element.41.low_hbm, ...), custom_call_target="tpu_custom_call" | custom-call | flops 9663676416 | bytes 31457280 | tf_op jit(solution)/shard_map/leave/pallas_call | solution.py:1214
  384.4 1.8 slice.42
  386.2 1.5 slice_bitcast_fusion.1
  387.7 1.0 reshape.40
  388.7 0.8 copy.37
  389.5 1.8 reshape.41
  391.3 2.7 copy.40
  393.9 1.7 copy.41
  (12 shorter events, 0.0 us)
Async XLA Ops:
  0.6 143.6 %collective-permute-start = (bf16[1024,768]{1,0:T(8,128)(2,1)}, bf16[1024,768]{1,0:T(8,128)(2,1)S(1)}, u32[]{:S(2)}, u32[]{:S(2)}) collective-permute-start(bf16[1024,768]{1,0:T(8,128)(2,1)} %d_ref.1), channel_id=1, source_target_pairs={{1,2},{2,1},{5,6},{6,5},{9,10},{10,9},{13,14},{14,13},{17,18},{18,... | collective-permute-start | bytes 4718600 | tf_op jit(solution)/shard_map/ppermute | solution.py:1536
  144.2 1.1 copy-start.3
  145.4 75.2 %copy-start.1 = (s32[2048]{0:T(1024)S(1)}, s32[2048]{0:T(1024)}, u32[]{:S(2)}) copy-start(s32[2048]{0:T(1024)} %param.15) | copy-start | bytes 24580
  219.5 8.0 %collective-permute-start.1 = (bf16[1024,384]{1,0:T(8,128)(2,1)}, bf16[1024,384]{1,0:T(8,128)(2,1)S(1)}, u32[]{:S(2)}, u32[]{:S(2)}) collective-permute-start(bf16[1024,384]{1,0:T(8,128)(2,1)} %get-tuple-element.36), channel_id=1, source_target_pairs={{0,2},{2,0},{1,3},{3,1},{4,6},{6,4},{5,7},{7,5},{8,10},{10,8},{9,1... | collective-permute-start | bytes 2359304 | tf_op jit(solution)/shard_map/ppermute | solution.py:1542
  220.5 0.7 collective-permute-start.2
  223.2 107.0 %collective-permute-start.3 = (bf16[1024,768]{1,0:T(8,128)(2,1)}, bf16[1024,768]{1,0:T(8,128)(2,1)S(1)}, u32[]{:S(2)}, u32[]{:S(2)}) collective-permute-start(bf16[1024,768]{1,0:T(8,128)(2,1)} %get-tuple-element.41.low_hbm), channel_id=1, source_target_pairs={{0,2},{2,0},{1,3},{3,1},{4,6},{6,4},{5,7},{7,5},{8,10},{10,8},{9,1... | collective-permute-start | bytes 4718600 | tf_op jit(solution)/shard_map/ppermute | solution.py:1542
  227.5 0.9 copy-start.4
  330.2 1.1 copy-start.2
  384.4 9.5 %copy-start = (f32[1024,768]{1,0:T(8,128)S(1)}, f32[1024,768]{1,0:T(8,128)}, u32[]{:S(2)}) copy-start(f32[1024,768]{1,0:T(8,128)} %get-tuple-element.70) | copy-start | bytes 9437188

commit v2 on v1

--- a/solution.py
+++ b/solution.py
@@ -1125,7 +1125,8 @@
     low_in_hbm,
     weights_hbm,
     grad_hbm,
-    sums_ref,
+    qkv_grad_ref,
+    out_grad_ref,
     grad_ref,
     o_ref,
     low_ref,
@@ -1141,6 +1142,7 @@
     mate_recv,
     cross_send,
     cross_recv,
+    sums_ref,
     *scratch,
 ):
     a, b, core, y = place()
@@ -1202,6 +1204,11 @@
         grad_ref[...] = total[...]
 
     reduce.end()
+    for pair in range(wide // (3 * LANES)):
+        for kind in range(3):
+            start = (pair * 3 + kind) * LANES
+            qkv_grad_ref[kind, :, pair * LANES : (pair + 1) * LANES] = sums_ref[:, start : start + LANES]
+    out_grad_ref[...] = sums_ref[:, wide:]
 
 
 def leave(back, done, o, low, low_in, weights, grad_one, collective_id):
@@ -1214,9 +1221,10 @@
     return pl.pallas_call(
         leave_kernel,
         in_specs=[vmem] + [anywhere] * 6,
-        out_specs=[vmem] * 2,
+        out_specs=[vmem] * 3,
         out_shape=[
-            jax.ShapeDtypeStruct((rows, wide + out_wide), F32),
+            jax.ShapeDtypeStruct((3, rows, wide // 3), F32),
+            jax.ShapeDtypeStruct((rows, out_wide), F32),
             jax.ShapeDtypeStruct((half, width), F32),
         ],
         scratch_shapes=[
@@ -1234,6 +1242,7 @@
             dma,
             dma((LINE,)),
             dma((LINE,)),
+            pltpu.VMEM((rows, wide + out_wide), F32),
             *Reduce.scratch(rows, wide + out_wide, FIRST_TILES * LANES),
         ],
         compiler_params=pltpu.CompilerParams(
@@ -1548,7 +1557,7 @@
     turn = core * half_len
 
     attn_shard = w_qkv.reshape(3, shard, pairs, LANES).transpose(1, 2, 0, 3).reshape(shard, 3 * half_cols)
-    vectors = jnp.stack([first_gain, first_bias, second_gain, second_bias], axis=1)
+    vectors = jnp.stack([first_gain, first_bias, second_gain, second_bias]).T
     pad = jnp.zeros((shard, LANES - 4), BF16)
     ff_shard = jnp.concatenate([w_gate, w_up, w_down.T, w_out.T, vectors, pad], axis=1)
     labels = cross(segments)
@@ -1573,7 +1582,7 @@
         qkv, o, do, do_in, lse, labels, cos, sin, rows_all, ff_sum, devices, 2
     )
     if devices == 8 * LINE:
-        attn_grad, grad_inputs = leave(
+        grad_qkv, grad_out, grad_inputs = leave(
             back, weight_grad, o, grad_one_low, grad_low_in, attn_w, grad_one, 3
         )
     else:
@@ -1581,26 +1590,26 @@
         attn_sum = jnp.concatenate([weight_grad, grad_out_t], axis=1)
         attn_sum = jnp.where(jnp.arange(2)[:, None, None] == core, attn_sum[None], 0)
         attn_grad = scatter_sum(attn_sum)
+        grad_qkv = (
+            attn_grad[:, : 3 * half_cols]
+            .reshape(shard, pairs, 3, LANES)
+            .transpose(2, 0, 1, 3)
+            .reshape(3, shard, half_cols)
+        )
+        grad_out = attn_grad[:, 3 * half_cols :]
         grad_rows = dot(back, lax.dynamic_index_in_dim(attn_w, core, 0, False), NT)
         grad_rows = grad_rows[:half_len] + mate(grad_rows[half_len:].astype(BF16)).astype(F32)
         grad_inputs = grad_one + grad_rows
         grad_inputs = jnp.where(moves, cross_in(grad_inputs.astype(BF16)).astype(F32), grad_inputs)
         outputs = cross(outputs)
 
-    grad_qkv = (
-        attn_grad[:, : 3 * half_cols]
-        .reshape(shard, pairs, 3, LANES)
-        .transpose(2, 0, 1, 3)
-        .reshape(3, shard, half_cols)
-    )
-    grad_out = attn_grad[:, 3 * half_cols :].T
     grad_gate, grad_up, grad_down_t = (ff_grad[:, k * half_ff : (k + 1) * half_ff] for k in range(3))
     grad_vectors = ff_grad[:, 3 * half_ff : 3 * half_ff + 4]
     return (
         outputs,
         grad_inputs,
         grad_qkv,
-        grad_out,
+        grad_out.T,
         grad_vectors[:, 0],
         grad_vectors[:, 1],
         grad_gate,

time: 400 us -> 394 us (0.985)
  local copies, waits for them, and re-layouts: 26.2 us -> 17.5 us
    unnamed x12 -> x20, local copies, waits for them, and re-layouts: 7.48 us -> 8.6 us
  transfers between devices with their start and end apart: 4 -> 4, of which waited for: 0 -> 0; matrix products, arithmetic and copies ran while one was open for 3% -> 3% of each run, Pallas kernels for 59% -> 61%
where the time goes in v2:
time: 394 us; the launch traced here: 390 us
  Pallas kernels  364 us (92%)
  local copies, waits for them, and re-layouts  17.5 us (4%)
  starting transfers between devices  6.72 us (2%)
    pallas_call x1, Pallas kernels, front(): pl.pallas_call(front_kernel, in_specs=[anywhere, anywhere, anywhere, vmem...  138 us
    pallas_call x1, Pallas kernels, attend_back(): pl.pallas_call(functools.partial(attend_back_kernel, remote=remote), in_s...  98.1 us
    pallas_call x1, Pallas kernels, feed(): pl.pallas_call(functools.partial(feed_kernel, blocks=blocks, remote=devic...  74.2 us
    pallas_call x1, Pallas kernels, leave(): pl.pallas_call(leave_kernel, in_specs=[vmem] + [anywhere] * 6, out_specs=...  53.2 us
    unnamed x20, local copies, waits for them, and re-layouts  8.6 us
  transfers between devices with their start and end apart: 4, of which 0 were waited for; matrix products, arithmetic and copies ran while one was open for 3% of the time, Pallas kernels for 61%

profile of v2, /device:TPU:0, one launch (start us, length us, event | category | flops | bytes accessed | tf_op | source)
XLA Modules:
  0.0 390.0 jit_solution(47637530505461810)
XLA Ops:
  0.6 0.8 collective-permute-start
  1.4 0.7 pad_maximum_fusion
  2.1 0.1 copy.37
  2.2 0.9 reshape.31
  3.2 0.1 copy.36
  3.3 0.7 reshape.32.attn_src
  4.0 1.9 concatenate.7.ff_src
  6.0 138.2 %front.1 = (bf16[2,768,1152]{2,1,0:T(8,128)(2,1)}, bf16[2048,768]{1,0:T(8,128)(2,1)}, bf16[2,768,5120]{2,1,0:T(8,128)(2,1)}, bf16[2048,1152]{1,0:T(8,128)(2,1)},...) custom-call(bf16[48,1152]{1,0:T(8,128)(2,1)} %reshape.32.attn_src, ...), custom_call_target="tpu_custom_call" | custom-call | flops 16508780544 | bytes 31457280 | tf_op jit(solution)/shard_map/front/pallas_call | solution.py:797
  144.2 0.0 collective-permute-done.d_in_ref
  144.2 0.0 copy-start.6
  144.2 1.1 copy-done.6
  145.4 74.2 %feed.1 = (bf16[1024,768]{1,0:T(8,128)(2,1)}, f32[1024,768]{1,0:T(8,128)}, bf16[1024,768]{1,0:T(8,128)(2,1)}, bf16[1024,384]{1,0:T(8,128)(2,1)}, bf16[1024,384]{...) custom-call(bf16[2048,768]{1,0:T(8,128)(2,1)} %get-tuple-element.30.x_ref.refs_9_, ...), custom_call_target="tpu_custom_call" | custom-call | flops 45902462976 | bytes 47185920 | tf_op jit(solution)/shard_map/feed/pallas_call | solution.py:1467
  219.5 1.0 collective-permute-start.1
  220.5 0.7 collective-permute-start.2
  221.2 0.0 collective-permute-done.2
  221.2 0.6 compare_select_fusion
  221.8 1.3 copy.38.refs_5_
  223.2 4.3 %collective-permute-start.3 = (bf16[1024,768]{1,0:T(8,128)(2,1)}, bf16[1024,768]{1,0:T(8,128)(2,1)S(1)}, u32[]{:S(2)}, u32[]{:S(2)}) collective-permute-start(bf16[1024,768]{1,0:T(8,128)(2,1)} %get-tuple-element.42.low_hbm), channel_id=1, source_target_pairs={{0,2},{2,0},{1,3},{3,1},{4,6},{6,4},{5,7},{7,5},{8,10},{10,8},{9,1... | collective-permute-start | bytes 4718600 | tf_op jit(solution)/shard_map/ppermute | solution.py:1551
  227.5 0.0 collective-permute-done.1.refs_3_
  227.5 0.9 copy-done.7
  228.4 98.1 %attend_back.1 = (bf16[2048,1152]{1,0:T(8,128)(2,1)}, bf16[768,1152]{1,0:T(8,128)(2,1)}, f32[48,4736]{1,0:T(8,128)}) custom-call(bf16[2048,1152]{1,0:T(8,128)(2,1)} %get-tuple-element.35.refs_0_, bf16[2048,384]{1,0:T(8,128)(2,1)} %get-tuple-element.31.o_ref.refs_1_.o_hbm, bf16[1024,384]{1,0:T(8,128)(2,1)} %get-tuple-element.36.refs_2_, ...), custom_call_target="tpu_custom_call" | custom-call | flops 32212254720 | bytes 18874368 | tf_op jit(solution)/shard_map/attend_back/pallas_call | solution.py:333
  326.5 1.7 slice_reduce_fusion
  328.2 2.1 slice_bitcast_fusion
  330.3 0.0 collective-permute-done.3.low_in_hbm
  330.3 1.1 copy-done.5
  331.4 53.2 %leave.1 = (f32[3,48,384]{2,1,0:T(8,128)}, f32[48,384]{1,0:T(8,128)}, f32[1024,768]{1,0:T(8,128)}) custom-call(bf16[2048,1152]{1,0:T(8,128)(2,1)} %get-tuple-element.40.back_ref, bf16[768,1152]{1,0:T(8,128)(2,1)} %get-tuple-element.41.done_hbm, bf16[2048,384]{1,0:T(8,128)(2,1)} %get-tuple-element.31.o_ref.refs_1_.o_hbm, ...), custom_call_target="tpu_custom_call" | custom-call | flops 9663676416 | bytes 31457280 | tf_op jit(solution)/shard_map/leave/pallas_call | solution.py:1221
  384.6 0.0 copy-start
  384.6 1.1 copy.43
  385.8 1.3 copy-done
  387.0 1.7 copy.44
  388.7 0.7 copy.45
  389.4 0.6 copy.46
  (13 shorter events, 0.0 us)
Async XLA Ops:
  0.6 143.6 %collective-permute-start = (bf16[1024,768]{1,0:T(8,128)(2,1)}, bf16[1024,768]{1,0:T(8,128)(2,1)S(1)}, u32[]{:S(2)}, u32[]{:S(2)}) collective-permute-start(bf16[1024,768]{1,0:T(8,128)(2,1)} %d_ref.1), channel_id=1, source_target_pairs={{1,2},{2,1},{5,6},{6,5},{9,10},{10,9},{13,14},{14,13},{17,18},{18,... | collective-permute-start | bytes 4718600 | tf_op jit(solution)/shard_map/ppermute | solution.py:1545
  144.2 1.1 copy-start.6
  145.4 75.2 %copy-start.4 = (s32[2048]{0:T(1024)S(1)}, s32[2048]{0:T(1024)}, u32[]{:S(2)}) copy-start(s32[2048]{0:T(1024)} %param.15) | copy-start | bytes 24580
  219.5 8.0 %collective-permute-start.1 = (bf16[1024,384]{1,0:T(8,128)(2,1)}, bf16[1024,384]{1,0:T(8,128)(2,1)S(1)}, u32[]{:S(2)}, u32[]{:S(2)}) collective-permute-start(bf16[1024,384]{1,0:T(8,128)(2,1)} %get-tuple-element.37), channel_id=1, source_target_pairs={{0,2},{2,0},{1,3},{3,1},{4,6},{6,4},{5,7},{7,5},{8,10},{10,8},{9,1... | collective-permute-start | bytes 2359304 | tf_op jit(solution)/shard_map/ppermute | solution.py:1551
  220.5 0.7 collective-permute-start.2
  223.2 107.1 %collective-permute-start.3 = (bf16[1024,768]{1,0:T(8,128)(2,1)}, bf16[1024,768]{1,0:T(8,128)(2,1)S(1)}, u32[]{:S(2)}, u32[]{:S(2)}) collective-permute-start(bf16[1024,768]{1,0:T(8,128)(2,1)} %get-tuple-element.42.low_hbm), channel_id=1, source_target_pairs={{0,2},{2,0},{1,3},{3,1},{4,6},{6,4},{5,7},{7,5},{8,10},{10,8},{9,1... | collective-permute-start | bytes 4718600 | tf_op jit(solution)/shard_map/ppermute | solution.py:1551
  227.5 0.9 copy-start.7
  330.3 1.1 copy-start.5
  331.4 53.2 %copy-start.1 = (bf16[1024,768]{1,0:T(8,128)(2,1)S(1)}, bf16[1024,768]{1,0:T(8,128)(2,1)}, u32[]{:S(2)}) copy-start(bf16[1024,768]{1,0:T(8,128)(2,1)} %get-tuple-element.71) | copy-start | bytes 4718596
  384.6 2.5 copy-start
  387.0 1.7 copy-start.2
  387.0 2.4 copy-start.3
